TPU v7x, 32 devices: a whole 2x2x4 slice. The times are simulated.
32 devices in a mesh: sgroup: 8 (over z, y), tile: 4 (over x, core).
Axes of the slice: x: 2, y: 2, z: 4, core: 2. Of those that a mesh axis runs over, the one named last changes fastest.
Arguments:
- voltages: bfloat16 [2, 128, 256, 2, 16, 128], P(None, 'sgroup', 'tile'), may hold values from -6 to 6
- weights: bfloat16 [2, 128, 256, 2, 16], P(None, 'sgroup'), may hold values from -0.25 to 0.25
- antenna_slot_index: int32 [128, 256], P('sgroup', 'tile'), may hold values from 0 to 255, each once within a row
- station_order: int32 [128], replicated, may hold values from 0 to 127, each once
Outputs:
- visibilities: float32 [16, 2, 256, 256], P('tile', None, 'sgroup')
Inputs may be any that keep to these rules, and one draw needn't show every extreme that they name: `station_order`: each station slot holds a different station. `antenna_slot_index`: within each station slot, each antenna slot holds a different antenna.
All inputs are finite; a program needn't handle non-finite values.
Results may differ from a plain program's by a relative error of at most 0.0038.
Values may be sent and summed in bfloat16 or wider, within the bound.
No kernel may reach another device: no remote copies, remote signals or barrier semaphores. Data moves between devices by JAX's collectives and lax.ppermute only.
A program may use at most 64 MiB of HBM per device.

v0:
```python
import functools

import jax
import jax.numpy as jnp
from jax import lax
from jax.experimental import pallas as pl
from jax.experimental.pallas import tpu as pltpu
from jax.sharding import PartitionSpec as P


F32, BF16 = jnp.float32, jnp.bfloat16


def iota(shape, axis):
    return lax.broadcasted_iota(jnp.int32, shape, axis)


def dot(left, right):
    return jnp.dot(left, right, preferred_element_type=F32)


def beam_kernel(owners, me_ref, index_hbm, w_hbm, v_hbm, keep_ref, send_ref, index_ref, w_ref, v_ref, left_ref, acc_ref, small_sem, v_sem):
    _, stations, antennas, polars, channels, spectra = v_ref.shape
    numbers = w_ref.shape[-1]
    per_owner = channels // owners
    rows = 2 * channels
    me = me_ref[0]
    together = 2 - stations % 2

    copies = [pltpu.make_async_copy(index_hbm, index_ref, small_sem.at[0]), pltpu.make_async_copy(w_hbm, w_ref, small_sem.at[1])]
    arrivals = [
        pltpu.make_async_copy(v_hbm.at[:, s : s + together], v_ref.at[:, s : s + together], v_sem.at[s])
        for s in range(0, stations, together)
    ]
    for copy in copies:
        copy.start(priority=0)
    for copy in arrivals:
        copy.start(priority=1)

    spread = jnp.where(iota((antennas, antennas * channels), 1) // channels == iota((antennas, antennas * channels), 0), 1.0, 0.0).astype(BF16)
    lane_tile = min(128, antennas * channels)
    mask = iota((rows, lane_tile), 1) % channels == iota((rows, lane_tile), 0) % channels
    number = iota((numbers, antennas), 0)
    for copy in copies:
        copy.wait()
    compact = []
    for s in range(stations):
        chosen = jnp.where(number == index_ref[s : s + 1, :], 1.0, 0.0).astype(BF16)
        lines = jnp.concatenate([w_ref[k, s, p] for p in range(polars) for k in range(2)], axis=0)
        compact.append(dot(lines, chosen).astype(BF16))
    for s in range(stations):
        wide = dot(compact[s], spread)
        for p in range(polars):
            for i in range(0, antennas * channels, lane_tile):
                part = wide[p * rows : (p + 1) * rows, i : i + lane_tile]
                left_ref[s, p, :, i : i + lane_tile] = jnp.where(mask, part, 0.0).astype(BF16)

    for s in range(stations):
        if s % together == 0:
            arrivals[s // together].wait()
        for p in range(polars):
            left = left_ref[s, p]
            real = dot(left, v_ref[0, s, :, p].reshape(antennas * channels, spectra))
            imag = dot(left, v_ref[1, s, :, p].reshape(antennas * channels, spectra))
            at = (s * polars + p) * rows
            acc_ref[at : at + channels, :] = real[:channels] - imag[channels:]
            acc_ref[at + channels : at + rows, :] = real[channels:] + imag[:channels]

    count = stations * polars
    for slot in range(owners):
        target = send_ref if slot % 2 else keep_ref
        first = (me ^ slot) * per_owner
        for part in range(2):
            for c in range(per_owner):
                line = acc_ref[pl.ds(first + part * channels + c, count, stride=rows), :]
                target[slot // 2, part * per_owner + c] = line.astype(target.dtype)


def beam(owners, me, index, weights, voltages):
    _, stations, antennas, polars, channels, spectra = voltages.shape
    rows = 2 * channels
    half = (owners // 2, rows // owners, stations * polars, spectra)
    hbm, vmem = pl.BlockSpec(memory_space=pltpu.HBM), pl.BlockSpec(memory_space=pltpu.VMEM)
    return pl.pallas_call(
        functools.partial(beam_kernel, owners),
        out_shape=(jax.ShapeDtypeStruct(half, F32), jax.ShapeDtypeStruct(half, F32)),
        in_specs=[pl.BlockSpec(memory_space=pltpu.SMEM), hbm, hbm, hbm],
        out_specs=[vmem, vmem],
        scratch_shapes=[
            pltpu.VMEM(index.shape, jnp.int32),
            pltpu.VMEM(weights.shape, BF16),
            pltpu.VMEM(voltages.shape, BF16),
            pltpu.VMEM((stations, polars, rows, antennas * channels), BF16),
            pltpu.VMEM((stations * polars * rows, spectra), F32),
            pltpu.SemaphoreType.DMA((2,)),
            pltpu.SemaphoreType.DMA((stations,)),
        ],
        compiler_params=pltpu.CompilerParams(vmem_limit_bytes=48 << 20),
        name="beam",
    )(me, *(pltpu.with_memory_space_constraint(a, pltpu.HBM) for a in (index, weights, voltages)))


def correlate_kernel(me_ref, order_ref, *refs):
    blocks, out_ref, row_ref = refs[:-2], refs[-2], refs[-1]
    groups = len(blocks)
    inner, local, spectra = blocks[0].shape
    channels = inner // 2
    total = groups * local
    stations = order_ref.shape[1]
    here = local * stations // total
    me = me_ref[0]
    polars = total // stations
    number = iota((total, stations), 0) // polars
    owns = jnp.where(order_ref[...] == number, 1.0, 0.0).astype(BF16)
    column = iota((stations, total), 1)
    slot = ((column // local) ^ me) * here + (column % local) // polars
    slots = jnp.where(iota((stations, total), 0) == slot, 1.0, 0.0).astype(BF16)
    same = iota((total, total), 0) % polars == iota((total, total), 1) % polars
    place = jnp.where(same, dot(owns, slots), 0.0).astype(BF16)
    scale = 1.0 / spectra
    for c in range(channels):
        real = jnp.concatenate([b[c] for b in blocks], axis=0)
        imag = jnp.concatenate([b[channels + c] for b in blocks], axis=0)
        both = jnp.concatenate([real, imag], axis=1)
        ordered = dot(place, both).astype(BF16)
        row_ref[...] = ordered
        mine = row_ref[pl.ds(pl.multiple_of(me * local, local), local), :]
        left = jnp.concatenate(
            [mine, jnp.concatenate([mine[:, spectra:], -mine[:, :spectra]], axis=1)], axis=0
        )
        vis = lax.dot_general(left, ordered, (((1,), (1,)), ((), ())), preferred_element_type=F32) * scale
        out_ref[c, 0] = vis[:local]
        out_ref[c, 1] = vis[local:]


def correlate(me, order, blocks):
    inner, local, spectra = blocks[0].shape
    total = len(blocks) * local
    shape = (inner // 2, 2, local, total)
    vmem = pl.BlockSpec(memory_space=pltpu.VMEM)
    return pl.pallas_call(
        correlate_kernel,
        out_shape=jax.ShapeDtypeStruct(shape, F32),
        in_specs=[pl.BlockSpec(memory_space=pltpu.SMEM), vmem] + [vmem] * len(blocks),
        out_specs=vmem,
        scratch_shapes=[pltpu.VMEM((total, 2 * spectra), BF16)],
        compiler_params=pltpu.CompilerParams(vmem_limit_bytes=48 << 20),
        name="correlate",
    )(me, order[None, :], *blocks)


def body(groups, owners, voltages, weights, antenna_slot_index, station_order):
    group, tile = lax.axis_index("sgroup").astype(jnp.int32), lax.axis_index("tile").astype(jnp.int32)
    far = groups // 2

    def exchange(value, axis, size, bit):
        return lax.ppermute(value, axis, [(i, i ^ bit) for i in range(size)])

    def share(value, bit):
        return exchange(value, "sgroup", groups, bit)

    keep, send = beam(owners, tile[None], antenna_slot_index, jnp.transpose(weights, (0, 1, 3, 4, 2)), voltages)
    total = keep + exchange(send, "tile", owners, 1)
    bit = 2
    while bit < owners:
        sent = exchange(total[1::2].astype(BF16), "tile", owners, bit)
        total = total[0::2] + sent.astype(F32)
        bit *= 2
    own = total[0].astype(BF16)
    blocks = {0: own, far: share(own, far)}
    for i in range(far - 2, 0, -1):
        blocks[i] = share(own, i)
    both = share(jnp.stack([own, blocks[far]]), far - 1)
    blocks[far - 1], blocks[far + far - 1] = both[0], both[1]
    for i in range(1, far - 1):
        blocks[far + i] = share(blocks[far], i)
    return correlate(group[None], station_order, [blocks[i] for i in range(groups)])


def solution(mesh):
    groups = mesh.shape["sgroup"]
    in_specs = (
        P(None, "sgroup", "tile", None, None, None),
        P(None, "sgroup", None, None, None),
        P("sgroup", "tile"),
        P(),
    )
    run = functools.partial(body, groups, mesh.shape["tile"])
    return jax.shard_map(run, mesh=mesh, in_specs=in_specs, out_specs=P("tile", None, "sgroup", None), check_vma=False)
```

profile of v0, /device:TPU:0, one launch (start us, length us, event | category | flops | bytes accessed | tf_op | source)
XLA Modules:
  0.0 30.4 jit_solution(15000399983945144131)
XLA Ops:
  0.0 0.0 copy-start
  0.0 6.9 %beam.1 = (f32[2,8,32,128]{3,2,1,0:T(8,128)S(1)}, f32[2,8,32,128]{3,2,1,0:T(8,128)S(1)}) custom-call(s32[1]{0:T(128)} %bitcast.2.me_ref, s32[16,64]{1,0:T(8,128)} %index_hbm.1, bf16[2,16,2,16,256]{4,3,2,1,0:T(8,128)(2,1)} %bitcast.16, bf16[2,16,64,2,16,128]{5,4,3,2,1,0:T(8,128)(2,1)} %v_hbm.1), custom_call_target="tpu_custom_call" | custom-call | tf_op jit(solution)/shard_map/beam/pallas_call | solution.py:84
  6.9 0.6 %collective-permute-start = (f32[2,8,32,128]{3,2,1,0:T(8,128)S(1)}, f32[2,8,32,128]{3,2,1,0:T(8,128)S(1)}, u32[]{:S(2)}, u32[]{:S(2)}) collective-permute-start(f32[2,8,32,128]{3,2,1,0:T(8,128)S(1)} %get-tuple-element.8), channel_id=1, source_target_pairs={{0,1},{1,0},{2,3},{3,2},{4,5},{5,4},{6,7},{7,6},{8,9},{9,8},{10,11... | collective-permute-start | bytes 786440 | tf_op jit(solution)/shard_map/ppermute | solution.py:157
  7.5 1.2 %collective-permute-done = f32[2,8,32,128]{3,2,1,0:T(8,128)S(1)} collective-permute-done((f32[2,8,32,128]{3,2,1,0:T(8,128)S(1)}, f32[2,8,32,128]{3,2,1,0:T(8,128)S(1)}, u32[]{:S(2)}, u32[]{:S(2)}) %collective-permute-start) | collective-permute-done | bytes 262176 | tf_op jit(solution)/shard_map/ppermute | solution.py:157
  8.7 2.9 %collective-permute-start.1 = (bf16[1,8,32,128]{3,2,1,0:T(8,128)(2,1)S(1)}, bf16[1,8,32,128]{3,2,1,0:T(8,128)(2,1)S(1)}, u32[]{:S(2)}, u32[]{:S(2)}) collective-permute-start(bf16[1,8,32,128]{3,2,1,0:T(8,128)(2,1)S(1)} %slice.29), channel_id=1, source_target_pairs={{0,2},{1,3},{2,0},{3,1},{4,6},{5,7},{6,4},{7,5},{8,10},{9,11},{10,... | collective-permute-start | bytes 196616 | tf_op jit(solution)/shard_map/ppermute | solution.py:157
  11.6 2.4 %collective-permute-done.1 = bf16[1,8,32,128]{3,2,1,0:T(8,128)(2,1)S(1)} collective-permute-done((bf16[1,8,32,128]{3,2,1,0:T(8,128)(2,1)S(1)}, bf16[1,8,32,128]{3,2,1,0:T(8,128)(2,1)S(1)}, u32[]{:S(2)}, u32[]{:S(2)}) %collective-permute-start.1) | collective-permute-done | bytes 65568 | tf_op jit(solution)/shard_map/ppermute | solution.py:157
  14.0 3.0 %collective-permute-start.4 = (bf16[8,32,128]{2,1,0:T(8,128)(2,1)S(1)}, bf16[8,32,128]{2,1,0:T(8,128)(2,1)S(1)}, u32[]{:S(2)}, u32[]{:S(2)}) collective-permute-start(bf16[8,32,128]{2,1,0:T(8,128)(2,1)S(1)} %bitcast.10), channel_id=1, source_target_pairs={{0,16},{4,20},{8,24},{12,28},{16,0},{20,4},{24,8},{28,12},{1,17},{... | collective-permute-start | bytes 196616 | tf_op jit(solution)/shard_map/ppermute | solution.py:157
  17.1 2.3 %collective-permute-done.4.refs_4_ = bf16[8,32,128]{2,1,0:T(8,128)(2,1)S(1)} collective-permute-done((bf16[8,32,128]{2,1,0:T(8,128)(2,1)S(1)}, bf16[8,32,128]{2,1,0:T(8,128)(2,1)S(1)}, u32[]{:S(2)}, u32[]{:S(2)}) %collective-permute-start.4) | collective-permute-done | bytes 65568 | tf_op jit(solution)/shard_map/ppermute | solution.py:157
  19.4 2.9 %collective-permute-start.5 = (bf16[2,8,32,128]{3,2,1,0:T(8,128)(2,1)S(1)}, bf16[2,8,32,128]{3,2,1,0:T(8,128)(2,1)S(1)}, u32[]{:S(2)}, u32[]{:S(2)}) collective-permute-start(bf16[2,8,32,128]{3,2,1,0:T(8,128)(2,1)S(1)} %pad_maximum_fusion), channel_id=1, source_target_pairs={{0,12},{4,8},{8,4},{12,0},{16,28},{20,24},{24,20},{28,16},{1,13},{... | collective-permute-start | bytes 393224 | tf_op jit(solution)/shard_map/ppermute | solution.py:157
  22.3 0.5 %collective-permute-start.3 = (bf16[8,32,128]{2,1,0:T(8,128)(2,1)S(1)}, bf16[8,32,128]{2,1,0:T(8,128)(2,1)S(1)}, u32[]{:S(2)}, u32[]{:S(2)}) collective-permute-start(bf16[8,32,128]{2,1,0:T(8,128)(2,1)S(1)} %bitcast.11), channel_id=1, source_target_pairs={{0,8},{4,12},{8,0},{12,4},{16,24},{20,28},{24,16},{28,20},{1,9},{5... | collective-permute-start | bytes 196616 | tf_op jit(solution)/shard_map/ppermute | solution.py:157
  22.7 0.2 collective-permute-start.2
  22.9 1.8 %collective-permute-start.7 = (bf16[8,32,128]{2,1,0:T(8,128)(2,1)S(1)}, bf16[8,32,128]{2,1,0:T(8,128)(2,1)S(1)}, u32[]{:S(2)}, u32[]{:S(2)}) collective-permute-start(bf16[8,32,128]{2,1,0:T(8,128)(2,1)S(1)} %collective-permute-done.4.refs_4_), channel_id=1, source_target_pairs={{0,8},{4,12},{8,0},{12,4},{16,24},{20,28},{24,16},{28,20},{1,9},{5... | collective-permute-start | bytes 196616 | tf_op jit(solution)/shard_map/ppermute | solution.py:157
  24.8 1.5 %collective-permute-start.6 = (bf16[8,32,128]{2,1,0:T(8,128)(2,1)S(1)}, bf16[8,32,128]{2,1,0:T(8,128)(2,1)S(1)}, u32[]{:S(2)}, u32[]{:S(2)}) collective-permute-start(bf16[8,32,128]{2,1,0:T(8,128)(2,1)S(1)} %collective-permute-done.4.refs_4_), channel_id=1, source_target_pairs={{0,4},{4,0},{8,12},{12,8},{16,20},{20,16},{24,28},{28,24},{1,5},{5... | collective-permute-start | bytes 196616 | tf_op jit(solution)/shard_map/ppermute | solution.py:157
  26.3 0.0 collective-permute-done.5
  26.3 0.2 collective-permute-done.3.refs_2_
  26.5 0.5 %collective-permute-done.2.refs_1_ = bf16[8,32,128]{2,1,0:T(8,128)(2,1)S(1)} collective-permute-done((bf16[8,32,128]{2,1,0:T(8,128)(2,1)S(1)}, bf16[8,32,128]{2,1,0:T(8,128)(2,1)S(1)}, u32[]{:S(2)}, u32[]{:S(2)}) %collective-permute-start.2) | collective-permute-done | bytes 65568 | tf_op jit(solution)/shard_map/ppermute | solution.py:157
  27.0 0.2 collective-permute-done.7.refs_6_
  27.2 1.8 %collective-permute-done.6.refs_5_ = bf16[8,32,128]{2,1,0:T(8,128)(2,1)S(1)} collective-permute-done((bf16[8,32,128]{2,1,0:T(8,128)(2,1)S(1)}, bf16[8,32,128]{2,1,0:T(8,128)(2,1)S(1)}, u32[]{:S(2)}, u32[]{:S(2)}) %collective-permute-start.6) | collective-permute-done | bytes 65568 | tf_op jit(solution)/shard_map/ppermute | solution.py:157
  29.1 0.0 copy-done
  29.1 1.4 %correlate.1 = f32[4,2,32,256]{3,2,1,0:T(8,128)} custom-call(s32[1]{0:T(128)} %bitcast.me_ref, s32[1,128]{1,0:T(1,128)S(1)} %bitcast.15, bf16[8,32,128]{2,1,0:T(8,128)(2,1)S(1)} %bitcast.13, bf16[8,32,128]{2,1,0:T(8,128)(2,1)S(1)} %collective-permute-done.2.refs_1_, bf16[8,32,128]{2,1,0:T(8,128)(2,1)S(1)} %collective-permute-done.3.refs_2_, ...), custom_call_target="tpu_custom_call" | custom-call | tf_op jit(solution)/shard_map/correlate/pallas_call | solution.py:141
  (5 shorter events, 0.1 us)
Async XLA Ops:
  0.0 29.1 %copy-start = (s32[128]{0:T(128)S(1)}, s32[128]{0:T(128)}, u32[]{:S(2)}) copy-start(s32[128]{0:T(128)} %param.7) | copy-start | bytes 1540
  6.9 1.7 %collective-permute-start = (f32[2,8,32,128]{3,2,1,0:T(8,128)S(1)}, f32[2,8,32,128]{3,2,1,0:T(8,128)S(1)}, u32[]{:S(2)}, u32[]{:S(2)}) collective-permute-start(f32[2,8,32,128]{3,2,1,0:T(8,128)S(1)} %get-tuple-element.8), channel_id=1, source_target_pairs={{0,1},{1,0},{2,3},{3,2},{4,5},{5,4},{6,7},{7,6},{8,9},{9,8},{10,11... | collective-permute-start | bytes 786440 | tf_op jit(solution)/shard_map/ppermute | solution.py:157
  8.7 5.3 %collective-permute-start.1 = (bf16[1,8,32,128]{3,2,1,0:T(8,128)(2,1)S(1)}, bf16[1,8,32,128]{3,2,1,0:T(8,128)(2,1)S(1)}, u32[]{:S(2)}, u32[]{:S(2)}) collective-permute-start(bf16[1,8,32,128]{3,2,1,0:T(8,128)(2,1)S(1)} %slice.29), channel_id=1, source_target_pairs={{0,2},{1,3},{2,0},{3,1},{4,6},{5,7},{6,4},{7,5},{8,10},{9,11},{10,... | collective-permute-start | bytes 196616 | tf_op jit(solution)/shard_map/ppermute | solution.py:157
  14.0 5.3 %collective-permute-start.4 = (bf16[8,32,128]{2,1,0:T(8,128)(2,1)S(1)}, bf16[8,32,128]{2,1,0:T(8,128)(2,1)S(1)}, u32[]{:S(2)}, u32[]{:S(2)}) collective-permute-start(bf16[8,32,128]{2,1,0:T(8,128)(2,1)S(1)} %bitcast.10), channel_id=1, source_target_pairs={{0,16},{4,20},{8,24},{12,28},{16,0},{20,4},{24,8},{28,12},{1,17},{... | collective-permute-start | bytes 196616 | tf_op jit(solution)/shard_map/ppermute | solution.py:157
  19.4 6.9 %collective-permute-start.5 = (bf16[2,8,32,128]{3,2,1,0:T(8,128)(2,1)S(1)}, bf16[2,8,32,128]{3,2,1,0:T(8,128)(2,1)S(1)}, u32[]{:S(2)}, u32[]{:S(2)}) collective-permute-start(bf16[2,8,32,128]{3,2,1,0:T(8,128)(2,1)S(1)} %pad_maximum_fusion), channel_id=1, source_target_pairs={{0,12},{4,8},{8,4},{12,0},{16,28},{20,24},{24,20},{28,16},{1,13},{... | collective-permute-start | bytes 393224 | tf_op jit(solution)/shard_map/ppermute | solution.py:157
  22.3 4.3 %collective-permute-start.3 = (bf16[8,32,128]{2,1,0:T(8,128)(2,1)S(1)}, bf16[8,32,128]{2,1,0:T(8,128)(2,1)S(1)}, u32[]{:S(2)}, u32[]{:S(2)}) collective-permute-start(bf16[8,32,128]{2,1,0:T(8,128)(2,1)S(1)} %bitcast.11), channel_id=1, source_target_pairs={{0,8},{4,12},{8,0},{12,4},{16,24},{20,28},{24,16},{28,20},{1,9},{5... | collective-permute-start | bytes 196616 | tf_op jit(solution)/shard_map/ppermute | solution.py:157
  22.7 4.3 %collective-permute-start.2 = (bf16[8,32,128]{2,1,0:T(8,128)(2,1)S(1)}, bf16[8,32,128]{2,1,0:T(8,128)(2,1)S(1)}, u32[]{:S(2)}, u32[]{:S(2)}) collective-permute-start(bf16[8,32,128]{2,1,0:T(8,128)(2,1)S(1)} %bitcast.12), channel_id=1, source_target_pairs={{0,4},{4,0},{8,12},{12,8},{16,20},{20,16},{24,28},{28,24},{1,5},{5... | collective-permute-start | bytes 196616 | tf_op jit(solution)/shard_map/ppermute | solution.py:157
  22.9 4.3 %collective-permute-start.7 = (bf16[8,32,128]{2,1,0:T(8,128)(2,1)S(1)}, bf16[8,32,128]{2,1,0:T(8,128)(2,1)S(1)}, u32[]{:S(2)}, u32[]{:S(2)}) collective-permute-start(bf16[8,32,128]{2,1,0:T(8,128)(2,1)S(1)} %collective-permute-done.4.refs_4_), channel_id=1, source_target_pairs={{0,8},{4,12},{8,0},{12,4},{16,24},{20,28},{24,16},{28,20},{1,9},{5... | collective-permute-start | bytes 196616 | tf_op jit(solution)/shard_map/ppermute | solution.py:157
  24.8 4.3 %collective-permute-start.6 = (bf16[8,32,128]{2,1,0:T(8,128)(2,1)S(1)}, bf16[8,32,128]{2,1,0:T(8,128)(2,1)S(1)}, u32[]{:S(2)}, u32[]{:S(2)}) collective-permute-start(bf16[8,32,128]{2,1,0:T(8,128)(2,1)S(1)} %collective-permute-done.4.refs_4_), channel_id=1, source_target_pairs={{0,4},{4,0},{8,12},{12,8},{16,20},{20,16},{24,28},{28,24},{1,5},{5... | collective-permute-start | bytes 196616 | tf_op jit(solution)/shard_map/ppermute | solution.py:157
where the time goes:
time: 30.6 us; the launch traced here: 30.4 us
  starting transfers between devices  13.4 us (44%)
  waiting for transfers between devices  8.59 us (28%)
  Pallas kernels  8.28 us (27%)
    ppermute x8, starting transfers between devices, exchange(): return lax.ppermute(value, axis, [(i, i ^ bit) for i in range(size)])  13.4 us
    ppermute x8, waiting for transfers between devices, exchange(): return lax.ppermute(value, axis, [(i, i ^ bit) for i in range(size)])  8.59 us
    pallas_call x1, Pallas kernels, beam(): pl.pallas_call(functools.partial(beam_kernel, owners), out_shape=(jax.Sha...  6.91 us
    pallas_call x1, Pallas kernels, correlate(): pl.pallas_call(correlate_kernel, out_shape=jax.ShapeDtypeStruct(shape, F3...  1.38 us
  transfers between devices with their start and end apart: 8, of which 7 were waited for; matrix products, arithmetic and copies ran while one was open for 0% of the time, Pallas kernels for 0%

commit v1 on v0

--- a/solution.py
+++ b/solution.py
@@ -25,16 +25,12 @@
     per_owner = channels // owners
     rows = 2 * channels
     me = me_ref[0]
-    together = 2 - stations % 2
-
     copies = [pltpu.make_async_copy(index_hbm, index_ref, small_sem.at[0]), pltpu.make_async_copy(w_hbm, w_ref, small_sem.at[1])]
-    arrivals = [
-        pltpu.make_async_copy(v_hbm.at[:, s : s + together], v_ref.at[:, s : s + together], v_sem.at[s])
-        for s in range(0, stations, together)
-    ]
+    spans = [(s, min(s + 2, stations)) for s in range(0, stations - 2, 2)] + [(s, s + 1) for s in range(max(stations - 2, 0), stations)]
+    arrivals = {a: pltpu.make_async_copy(v_hbm.at[:, a:b], v_ref.at[:, a:b], v_sem.at[a]) for a, b in spans}
     for copy in copies:
         copy.start(priority=0)
-    for copy in arrivals:
+    for copy in arrivals.values():
         copy.start(priority=1)
 
     spread = jnp.where(iota((antennas, antennas * channels), 1) // channels == iota((antennas, antennas * channels), 0), 1.0, 0.0).astype(BF16)
@@ -55,9 +51,19 @@
                 part = wide[p * rows : (p + 1) * rows, i : i + lane_tile]
                 left_ref[s, p, :, i : i + lane_tile] = jnp.where(mask, part, 0.0).astype(BF16)
 
+    def order_rows(stop, size):
+        for slot in range(owners):
+            target = send_ref if slot % 2 else keep_ref
+            first = (stop - size) * polars * rows + (me ^ slot) * per_owner
+            for part in range(2):
+                for c in range(per_owner):
+                    line = acc_ref[pl.ds(first + part * channels + c, size * polars, stride=rows), :]
+                    target[slot // 2, part * per_owner + c, (stop - size) * polars : stop * polars] = line
+
+    batch = 4 if stations % 4 == 0 else stations
     for s in range(stations):
-        if s % together == 0:
-            arrivals[s // together].wait()
+        if s in arrivals:
+            arrivals[s].wait()
         for p in range(polars):
             left = left_ref[s, p]
             real = dot(left, v_ref[0, s, :, p].reshape(antennas * channels, spectra))
@@ -65,15 +71,8 @@
             at = (s * polars + p) * rows
             acc_ref[at : at + channels, :] = real[:channels] - imag[channels:]
             acc_ref[at + channels : at + rows, :] = real[channels:] + imag[:channels]
-
-    count = stations * polars
-    for slot in range(owners):
-        target = send_ref if slot % 2 else keep_ref
-        first = (me ^ slot) * per_owner
-        for part in range(2):
-            for c in range(per_owner):
-                line = acc_ref[pl.ds(first + part * channels + c, count, stride=rows), :]
-                target[slot // 2, part * per_owner + c] = line.astype(target.dtype)
+        if (s + 1) % batch == 0:
+            order_rows(s + 1, batch)
 
 
 def beam(owners, me, index, weights, voltages):
@@ -100,40 +99,55 @@
     )(me, *(pltpu.with_memory_space_constraint(a, pltpu.HBM) for a in (index, weights, voltages)))
 
 
-def correlate_kernel(me_ref, order_ref, *refs):
-    blocks, out_ref, row_ref = refs[:-2], refs[-2], refs[-1]
-    groups = len(blocks)
+def place_kernel(local, polars, me_ref, order_ref, place_ref):
+    total, stations = place_ref.shape[0], order_ref.shape[1]
+    owns = jnp.where(order_ref[...] == iota((total, stations), 0) // polars, 1.0, 0.0).astype(BF16)
+    column = iota((stations, total), 1)
+    slot = ((column // local) ^ me_ref[0]) * (local // polars) + (column % local) // polars
+    slots = jnp.where(iota((stations, total), 0) == slot, 1.0, 0.0).astype(BF16)
+    same = iota((total, total), 0) % polars == iota((total, total), 1) % polars
+    place_ref[...] = jnp.where(same, dot(owns, slots), 0.0).astype(BF16)
+
+
+def placement(me, order, polars, local):
+    vmem = pl.BlockSpec(memory_space=pltpu.VMEM)
+    total = order.shape[0] * polars
+    return pl.pallas_call(
+        functools.partial(place_kernel, local, polars),
+        out_shape=jax.ShapeDtypeStruct((total, total), BF16),
+        in_specs=[pl.BlockSpec(memory_space=pltpu.SMEM), vmem],
+        out_specs=vmem,
+        compiler_params=pltpu.CompilerParams(vmem_limit_bytes=48 << 20),
+        name="place",
+    )(me, order[None, :])
+
+
+def correlate_kernel(me_ref, place_ref, *refs):
+    blocks, (out_hbm, row_ref, out_ref, sem) = refs[:-4], refs[-4:]
     inner, local, spectra = blocks[0].shape
     channels = inner // 2
-    total = groups * local
-    stations = order_ref.shape[1]
-    here = local * stations // total
-    me = me_ref[0]
-    polars = total // stations
-    number = iota((total, stations), 0) // polars
-    owns = jnp.where(order_ref[...] == number, 1.0, 0.0).astype(BF16)
-    column = iota((stations, total), 1)
-    slot = ((column // local) ^ me) * here + (column % local) // polars
-    slots = jnp.where(iota((stations, total), 0) == slot, 1.0, 0.0).astype(BF16)
-    same = iota((total, total), 0) % polars == iota((total, total), 1) % polars
-    place = jnp.where(same, dot(owns, slots), 0.0).astype(BF16)
+    me, place = me_ref[0], place_ref[...]
     scale = 1.0 / spectra
     for c in range(channels):
         real = jnp.concatenate([b[c] for b in blocks], axis=0)
         imag = jnp.concatenate([b[channels + c] for b in blocks], axis=0)
-        both = jnp.concatenate([real, imag], axis=1)
-        ordered = dot(place, both).astype(BF16)
-        row_ref[...] = ordered
-        mine = row_ref[pl.ds(pl.multiple_of(me * local, local), local), :]
+        row_ref[c] = dot(place, jnp.concatenate([real, imag], axis=1)).astype(BF16)
+    rows, copies = pl.ds(pl.multiple_of(me * local, local), local), []
+    for c in range(channels):
+        mine = row_ref[c, rows, :]
         left = jnp.concatenate(
             [mine, jnp.concatenate([mine[:, spectra:], -mine[:, :spectra]], axis=1)], axis=0
         )
-        vis = lax.dot_general(left, ordered, (((1,), (1,)), ((), ())), preferred_element_type=F32) * scale
+        vis = lax.dot_general(left, row_ref[c], (((1,), (1,)), ((), ())), preferred_element_type=F32) * scale
         out_ref[c, 0] = vis[:local]
         out_ref[c, 1] = vis[local:]
-
-
-def correlate(me, order, blocks):
+        copies.append(pltpu.make_async_copy(out_ref.at[c], out_hbm.at[c], sem.at[c]))
+        copies[-1].start()
+    for copy in copies:
+        copy.wait()
+
+
+def correlate(me, place, blocks):
     inner, local, spectra = blocks[0].shape
     total = len(blocks) * local
     shape = (inner // 2, 2, local, total)
@@ -142,11 +156,15 @@
         correlate_kernel,
         out_shape=jax.ShapeDtypeStruct(shape, F32),
         in_specs=[pl.BlockSpec(memory_space=pltpu.SMEM), vmem] + [vmem] * len(blocks),
-        out_specs=vmem,
-        scratch_shapes=[pltpu.VMEM((total, 2 * spectra), BF16)],
+        out_specs=pl.BlockSpec(memory_space=pltpu.HBM),
+        scratch_shapes=[
+            pltpu.VMEM((inner // 2, total, 2 * spectra), BF16),
+            pltpu.VMEM(shape, F32),
+            pltpu.SemaphoreType.DMA((inner // 2,)),
+        ],
         compiler_params=pltpu.CompilerParams(vmem_limit_bytes=48 << 20),
         name="correlate",
-    )(me, order[None, :], *blocks)
+    )(me, place, *blocks)
 
 
 def body(groups, owners, voltages, weights, antenna_slot_index, station_order):
@@ -174,7 +192,8 @@
     blocks[far - 1], blocks[far + far - 1] = both[0], both[1]
     for i in range(1, far - 1):
         blocks[far + i] = share(blocks[far], i)
-    return correlate(group[None], station_order, [blocks[i] for i in range(groups)])
+    place = placement(group[None], station_order, voltages.shape[3], own.shape[1])
+    return correlate(group[None], place, [blocks[i] for i in range(groups)])
 
 
 def solution(mesh):

time: 30.6 us -> 30.3 us (level)
  transfers between devices with their start and end apart: 8 -> 8, of which waited for: 7 -> 8; matrix products, arithmetic and copies ran while one was open for 0% -> 0% of each run, Pallas kernels for 0% -> 1%
where the time goes in v1:
time: 30.3 us; the launch traced here: 30.2 us
  starting transfers between devices  13.5 us (45%)
  waiting for transfers between devices  8.54 us (28%)
  Pallas kernels  8.02 us (26%)
    ppermute x8, starting transfers between devices, exchange(): return lax.ppermute(value, axis, [(i, i ^ bit) for i in range(size)])  13.5 us
    ppermute x8, waiting for transfers between devices, exchange(): return lax.ppermute(value, axis, [(i, i ^ bit) for i in range(size)])  8.54 us
    pallas_call x1, Pallas kernels, beam(): pl.pallas_call(functools.partial(beam_kernel, owners), out_shape=(jax.Sha...  6.64 us
    pallas_call x1, Pallas kernels, correlate(): pl.pallas_call(correlate_kernel, out_shape=jax.ShapeDtypeStruct(shape, F3...  1.21 us
  transfers between devices with their start and end apart: 8, of which 8 were waited for; matrix products, arithmetic and copies ran while one was open for 0% of the time, Pallas kernels for 1%

profile of v1, /device:TPU:0, one launch (start us, length us, event | category | flops | bytes accessed | tf_op | source)
XLA Modules:
  0.0 30.2 jit_solution(18331609210637631709)
XLA Ops:
  0.0 0.0 copy-start
  0.0 6.6 %beam.1 = (f32[2,8,32,128]{3,2,1,0:T(8,128)S(1)}, f32[2,8,32,128]{3,2,1,0:T(8,128)S(1)}) custom-call(s32[1]{0:T(128)} %bitcast.2.me_ref, s32[16,64]{1,0:T(8,128)} %index_hbm.1, bf16[2,16,2,16,256]{4,3,2,1,0:T(8,128)(2,1)} %bitcast.16, bf16[2,16,64,2,16,128]{5,4,3,2,1,0:T(8,128)(2,1)} %v_hbm.1), custom_call_target="tpu_custom_call" | custom-call | tf_op jit(solution)/shard_map/beam/pallas_call | solution.py:83
  6.6 0.6 %collective-permute-start = (f32[2,8,32,128]{3,2,1,0:T(8,128)S(1)}, f32[2,8,32,128]{3,2,1,0:T(8,128)S(1)}, u32[]{:S(2)}, u32[]{:S(2)}) collective-permute-start(f32[2,8,32,128]{3,2,1,0:T(8,128)S(1)} %get-tuple-element.8), channel_id=1, source_target_pairs={{0,1},{1,0},{2,3},{3,2},{4,5},{5,4},{6,7},{7,6},{8,9},{9,8},{10,11... | collective-permute-start | bytes 786440 | tf_op jit(solution)/shard_map/ppermute | solution.py:175
  7.2 1.2 %collective-permute-done = f32[2,8,32,128]{3,2,1,0:T(8,128)S(1)} collective-permute-done((f32[2,8,32,128]{3,2,1,0:T(8,128)S(1)}, f32[2,8,32,128]{3,2,1,0:T(8,128)S(1)}, u32[]{:S(2)}, u32[]{:S(2)}) %collective-permute-start) | collective-permute-done | bytes 262176 | tf_op jit(solution)/shard_map/ppermute | solution.py:175
  8.4 2.9 %collective-permute-start.1 = (bf16[1,8,32,128]{3,2,1,0:T(8,128)(2,1)S(1)}, bf16[1,8,32,128]{3,2,1,0:T(8,128)(2,1)S(1)}, u32[]{:S(2)}, u32[]{:S(2)}) collective-permute-start(bf16[1,8,32,128]{3,2,1,0:T(8,128)(2,1)S(1)} %slice.29), channel_id=1, source_target_pairs={{0,2},{1,3},{2,0},{3,1},{4,6},{5,7},{6,4},{7,5},{8,10},{9,11},{10,... | collective-permute-start | bytes 196616 | tf_op jit(solution)/shard_map/ppermute | solution.py:175
  11.3 2.4 %collective-permute-done.1 = bf16[1,8,32,128]{3,2,1,0:T(8,128)(2,1)S(1)} collective-permute-done((bf16[1,8,32,128]{3,2,1,0:T(8,128)(2,1)S(1)}, bf16[1,8,32,128]{3,2,1,0:T(8,128)(2,1)S(1)}, u32[]{:S(2)}, u32[]{:S(2)}) %collective-permute-start.1) | collective-permute-done | bytes 65568 | tf_op jit(solution)/shard_map/ppermute | solution.py:175
  13.8 3.0 %collective-permute-start.4 = (bf16[8,32,128]{2,1,0:T(8,128)(2,1)S(1)}, bf16[8,32,128]{2,1,0:T(8,128)(2,1)S(1)}, u32[]{:S(2)}, u32[]{:S(2)}) collective-permute-start(bf16[8,32,128]{2,1,0:T(8,128)(2,1)S(1)} %bitcast.10), channel_id=1, source_target_pairs={{0,16},{4,20},{8,24},{12,28},{16,0},{20,4},{24,8},{28,12},{1,17},{... | collective-permute-start | bytes 196616 | tf_op jit(solution)/shard_map/ppermute | solution.py:175
  16.8 2.3 %collective-permute-done.4.refs_4_ = bf16[8,32,128]{2,1,0:T(8,128)(2,1)S(1)} collective-permute-done((bf16[8,32,128]{2,1,0:T(8,128)(2,1)S(1)}, bf16[8,32,128]{2,1,0:T(8,128)(2,1)S(1)}, u32[]{:S(2)}, u32[]{:S(2)}) %collective-permute-start.4) | collective-permute-done | bytes 65568 | tf_op jit(solution)/shard_map/ppermute | solution.py:175
  19.1 2.9 %collective-permute-start.5 = (bf16[2,8,32,128]{3,2,1,0:T(8,128)(2,1)S(1)}, bf16[2,8,32,128]{3,2,1,0:T(8,128)(2,1)S(1)}, u32[]{:S(2)}, u32[]{:S(2)}) collective-permute-start(bf16[2,8,32,128]{3,2,1,0:T(8,128)(2,1)S(1)} %pad_maximum_fusion), channel_id=1, source_target_pairs={{0,12},{4,8},{8,4},{12,0},{16,28},{20,24},{24,20},{28,16},{1,13},{... | collective-permute-start | bytes 393224 | tf_op jit(solution)/shard_map/ppermute | solution.py:175
  22.0 0.0 copy-done
  22.0 0.2 place.1.place_ref
  22.2 0.6 %collective-permute-start.2 = (bf16[8,32,128]{2,1,0:T(8,128)(2,1)S(1)}, bf16[8,32,128]{2,1,0:T(8,128)(2,1)S(1)}, u32[]{:S(2)}, u32[]{:S(2)}) collective-permute-start(bf16[8,32,128]{2,1,0:T(8,128)(2,1)S(1)} %bitcast.11), channel_id=1, source_target_pairs={{0,4},{4,0},{8,12},{12,8},{16,20},{20,16},{24,28},{28,24},{1,5},{5... | collective-permute-start | bytes 196616 | tf_op jit(solution)/shard_map/ppermute | solution.py:175
  22.7 0.2 collective-permute-start.3
  22.9 1.8 %collective-permute-start.6 = (bf16[8,32,128]{2,1,0:T(8,128)(2,1)S(1)}, bf16[8,32,128]{2,1,0:T(8,128)(2,1)S(1)}, u32[]{:S(2)}, u32[]{:S(2)}) collective-permute-start(bf16[8,32,128]{2,1,0:T(8,128)(2,1)S(1)} %collective-permute-done.4.refs_4_), channel_id=1, source_target_pairs={{0,4},{4,0},{8,12},{12,8},{16,20},{20,16},{24,28},{28,24},{1,5},{5... | collective-permute-start | bytes 196616 | tf_op jit(solution)/shard_map/ppermute | solution.py:175
  24.7 1.6 %collective-permute-start.7 = (bf16[8,32,128]{2,1,0:T(8,128)(2,1)S(1)}, bf16[8,32,128]{2,1,0:T(8,128)(2,1)S(1)}, u32[]{:S(2)}, u32[]{:S(2)}) collective-permute-start(bf16[8,32,128]{2,1,0:T(8,128)(2,1)S(1)} %collective-permute-done.4.refs_4_), channel_id=1, source_target_pairs={{0,8},{4,12},{8,0},{12,4},{16,24},{20,28},{24,16},{28,20},{1,9},{5... | collective-permute-start | bytes 196616 | tf_op jit(solution)/shard_map/ppermute | solution.py:175
  26.3 0.1 collective-permute-done.5
  26.5 0.4 %collective-permute-done.2.refs_1_ = bf16[8,32,128]{2,1,0:T(8,128)(2,1)S(1)} collective-permute-done((bf16[8,32,128]{2,1,0:T(8,128)(2,1)S(1)}, bf16[8,32,128]{2,1,0:T(8,128)(2,1)S(1)}, u32[]{:S(2)}, u32[]{:S(2)}) %collective-permute-start.2) | collective-permute-done | bytes 65568 | tf_op jit(solution)/shard_map/ppermute | solution.py:175
  26.8 0.2 collective-permute-done.3.refs_2_
  27.0 0.5 %collective-permute-done.6.refs_5_ = bf16[8,32,128]{2,1,0:T(8,128)(2,1)S(1)} collective-permute-done((bf16[8,32,128]{2,1,0:T(8,128)(2,1)S(1)}, bf16[8,32,128]{2,1,0:T(8,128)(2,1)S(1)}, u32[]{:S(2)}, u32[]{:S(2)}) %collective-permute-start.6) | collective-permute-done | bytes 65568 | tf_op jit(solution)/shard_map/ppermute | solution.py:175
  27.5 1.5 %collective-permute-done.7.refs_6_ = bf16[8,32,128]{2,1,0:T(8,128)(2,1)S(1)} collective-permute-done((bf16[8,32,128]{2,1,0:T(8,128)(2,1)S(1)}, bf16[8,32,128]{2,1,0:T(8,128)(2,1)S(1)}, u32[]{:S(2)}, u32[]{:S(2)}) %collective-permute-start.7) | collective-permute-done | bytes 65568 | tf_op jit(solution)/shard_map/ppermute | solution.py:175
  29.0 1.2 %correlate.1 = f32[4,2,32,256]{3,2,1,0:T(8,128)} custom-call(s32[1]{0:T(128)} %bitcast.me_ref, bf16[256,256]{1,0:T(8,128)(2,1)S(1)} %place.1.place_ref, bf16[8,32,128]{2,1,0:T(8,128)(2,1)S(1)} %bitcast.13, bf16[8,32,128]{2,1,0:T(8,128)(2,1)S(1)} %collective-permute-done.2.refs_1_, bf16[8,32,128]{2,1,0:T(8,128)(2,1)S(1)} %collective-permute-done.3.refs_2_, ...), custom_call_target="tpu_custom_call" | custom-call | tf_op jit(solution)/shard_map/correlate/pallas_call | solution.py:155
  (5 shorter events, 0.1 us)
Async XLA Ops:
  0.0 22.0 %copy-start = (s32[128]{0:T(128)S(1)}, s32[128]{0:T(128)}, u32[]{:S(2)}) copy-start(s32[128]{0:T(128)} %param.7) | copy-start | bytes 1540
  6.6 1.7 %collective-permute-start = (f32[2,8,32,128]{3,2,1,0:T(8,128)S(1)}, f32[2,8,32,128]{3,2,1,0:T(8,128)S(1)}, u32[]{:S(2)}, u32[]{:S(2)}) collective-permute-start(f32[2,8,32,128]{3,2,1,0:T(8,128)S(1)} %get-tuple-element.8), channel_id=1, source_target_pairs={{0,1},{1,0},{2,3},{3,2},{4,5},{5,4},{6,7},{7,6},{8,9},{9,8},{10,11... | collective-permute-start | bytes 786440 | tf_op jit(solution)/shard_map/ppermute | solution.py:175
  8.4 5.3 %collective-permute-start.1 = (bf16[1,8,32,128]{3,2,1,0:T(8,128)(2,1)S(1)}, bf16[1,8,32,128]{3,2,1,0:T(8,128)(2,1)S(1)}, u32[]{:S(2)}, u32[]{:S(2)}) collective-permute-start(bf16[1,8,32,128]{3,2,1,0:T(8,128)(2,1)S(1)} %slice.29), channel_id=1, source_target_pairs={{0,2},{1,3},{2,0},{3,1},{4,6},{5,7},{6,4},{7,5},{8,10},{9,11},{10,... | collective-permute-start | bytes 196616 | tf_op jit(solution)/shard_map/ppermute | solution.py:175
  13.8 5.3 %collective-permute-start.4 = (bf16[8,32,128]{2,1,0:T(8,128)(2,1)S(1)}, bf16[8,32,128]{2,1,0:T(8,128)(2,1)S(1)}, u32[]{:S(2)}, u32[]{:S(2)}) collective-permute-start(bf16[8,32,128]{2,1,0:T(8,128)(2,1)S(1)} %bitcast.10), channel_id=1, source_target_pairs={{0,16},{4,20},{8,24},{12,28},{16,0},{20,4},{24,8},{28,12},{1,17},{... | collective-permute-start | bytes 196616 | tf_op jit(solution)/shard_map/ppermute | solution.py:175
  19.1 7.3 %collective-permute-start.5 = (bf16[2,8,32,128]{3,2,1,0:T(8,128)(2,1)S(1)}, bf16[2,8,32,128]{3,2,1,0:T(8,128)(2,1)S(1)}, u32[]{:S(2)}, u32[]{:S(2)}) collective-permute-start(bf16[2,8,32,128]{3,2,1,0:T(8,128)(2,1)S(1)} %pad_maximum_fusion), channel_id=1, source_target_pairs={{0,12},{4,8},{8,4},{12,0},{16,28},{20,24},{24,20},{28,16},{1,13},{... | collective-permute-start | bytes 393224 | tf_op jit(solution)/shard_map/ppermute | solution.py:175
  22.2 4.6 %collective-permute-start.2 = (bf16[8,32,128]{2,1,0:T(8,128)(2,1)S(1)}, bf16[8,32,128]{2,1,0:T(8,128)(2,1)S(1)}, u32[]{:S(2)}, u32[]{:S(2)}) collective-permute-start(bf16[8,32,128]{2,1,0:T(8,128)(2,1)S(1)} %bitcast.11), channel_id=1, source_target_pairs={{0,4},{4,0},{8,12},{12,8},{16,20},{20,16},{24,28},{28,24},{1,5},{5... | collective-permute-start | bytes 196616 | tf_op jit(solution)/shard_map/ppermute | solution.py:175
  22.7 4.3 %collective-permute-start.3 = (bf16[8,32,128]{2,1,0:T(8,128)(2,1)S(1)}, bf16[8,32,128]{2,1,0:T(8,128)(2,1)S(1)}, u32[]{:S(2)}, u32[]{:S(2)}) collective-permute-start(bf16[8,32,128]{2,1,0:T(8,128)(2,1)S(1)} %bitcast.12), channel_id=1, source_target_pairs={{0,8},{4,12},{8,0},{12,4},{16,24},{20,28},{24,16},{28,20},{1,9},{5... | collective-permute-start | bytes 196616 | tf_op jit(solution)/shard_map/ppermute | solution.py:175
  22.9 4.6 %collective-permute-start.6 = (bf16[8,32,128]{2,1,0:T(8,128)(2,1)S(1)}, bf16[8,32,128]{2,1,0:T(8,128)(2,1)S(1)}, u32[]{:S(2)}, u32[]{:S(2)}) collective-permute-start(bf16[8,32,128]{2,1,0:T(8,128)(2,1)S(1)} %collective-permute-done.4.refs_4_), channel_id=1, source_target_pairs={{0,4},{4,0},{8,12},{12,8},{16,20},{20,16},{24,28},{28,24},{1,5},{5... | collective-permute-start | bytes 196616 | tf_op jit(solution)/shard_map/ppermute | solution.py:175
  24.7 4.3 %collective-permute-start.7 = (bf16[8,32,128]{2,1,0:T(8,128)(2,1)S(1)}, bf16[8,32,128]{2,1,0:T(8,128)(2,1)S(1)}, u32[]{:S(2)}, u32[]{:S(2)}) collective-permute-start(bf16[8,32,128]{2,1,0:T(8,128)(2,1)S(1)} %collective-permute-done.4.refs_4_), channel_id=1, source_target_pairs={{0,8},{4,12},{8,0},{12,4},{16,24},{20,28},{24,16},{28,20},{1,9},{5... | collective-permute-start | bytes 196616 | tf_op jit(solution)/shard_map/ppermute | solution.py:175

commit v2 on v1

--- a/solution.py
+++ b/solution.py
@@ -58,7 +58,7 @@
             for part in range(2):
                 for c in range(per_owner):
                     line = acc_ref[pl.ds(first + part * channels + c, size * polars, stride=rows), :]
-                    target[slot // 2, part * per_owner + c, (stop - size) * polars : stop * polars] = line
+                    target[slot // 2, part * per_owner + c, (stop - size) * polars : stop * polars] = line.astype(target.dtype)
 
     batch = 4 if stations % 4 == 0 else stations
     for s in range(stations):
@@ -82,7 +82,7 @@
     hbm, vmem = pl.BlockSpec(memory_space=pltpu.HBM), pl.BlockSpec(memory_space=pltpu.VMEM)
     return pl.pallas_call(
         functools.partial(beam_kernel, owners),
-        out_shape=(jax.ShapeDtypeStruct(half, F32), jax.ShapeDtypeStruct(half, F32)),
+        out_shape=(jax.ShapeDtypeStruct(half, F32), jax.ShapeDtypeStruct(half, BF16)),
         in_specs=[pl.BlockSpec(memory_space=pltpu.SMEM), hbm, hbm, hbm],
         out_specs=[vmem, vmem],
         scratch_shapes=[
@@ -178,7 +178,7 @@
         return exchange(value, "sgroup", groups, bit)
 
     keep, send = beam(owners, tile[None], antenna_slot_index, jnp.transpose(weights, (0, 1, 3, 4, 2)), voltages)
-    total = keep + exchange(send, "tile", owners, 1)
+    total = keep + exchange(send, "tile", owners, 1).astype(F32)
     bit = 2
     while bit < owners:
         sent = exchange(total[1::2].astype(BF16), "tile", owners, bit)

time: 30.3 us -> 30.2 us (level)
  transfers between devices with their start and end apart: 8 -> 8, of which waited for: 8 -> 7; matrix products, arithmetic and copies ran while one was open for 0% -> 0% of each run, Pallas kernels for 1% -> 1%
where the time goes in v2:
time: 30.2 us; the launch traced here: 30.1 us
  starting transfers between devices  13.4 us (44%)
  waiting for transfers between devices  8.45 us (28%)
  Pallas kernels  8.03 us (27%)
    ppermute x8, starting transfers between devices, exchange(): return lax.ppermute(value, axis, [(i, i ^ bit) for i in range(size)])  13.4 us
    ppermute x8, waiting for transfers between devices, exchange(): return lax.ppermute(value, axis, [(i, i ^ bit) for i in range(size)])  8.45 us
    pallas_call x1, Pallas kernels, beam(): pl.pallas_call(functools.partial(beam_kernel, owners), out_shape=(jax.Sha...  6.64 us
    pallas_call x1, Pallas kernels, correlate(): pl.pallas_call(correlate_kernel, out_shape=jax.ShapeDtypeStruct(shape, F3...  1.21 us
  transfers between devices with their start and end apart: 8, of which 7 were waited for; matrix products, arithmetic and copies ran while one was open for 0% of the time, Pallas kernels for 1%

profile of v2, /device:TPU:0, one launch (start us, length us, event | category | flops | bytes accessed | tf_op | source)
XLA Modules:
  0.0 30.1 jit_solution(4667252760285127663)
XLA Ops:
  0.0 0.0 copy-start
  0.0 6.6 %beam.1 = (f32[2,8,32,128]{3,2,1,0:T(8,128)S(1)}, bf16[2,8,32,128]{3,2,1,0:T(8,128)(2,1)S(1)}) custom-call(s32[1]{0:T(128)} %bitcast.2.me_ref, s32[16,64]{1,0:T(8,128)} %index_hbm.1, bf16[2,16,2,16,256]{4,3,2,1,0:T(8,128)(2,1)} %bitcast.16, bf16[2,16,64,2,16,128]{5,4,3,2,1,0:T(8,128)(2,1)} %v_hbm.1), custom_call_target="tpu_custom_call" | custom-call | tf_op jit(solution)/shard_map/beam/pallas_call | solution.py:83
  6.7 0.6 %collective-permute-start = (bf16[2,8,32,128]{3,2,1,0:T(8,128)(2,1)S(1)}, bf16[2,8,32,128]{3,2,1,0:T(8,128)(2,1)S(1)}, u32[]{:S(2)}, u32[]{:S(2)}) collective-permute-start(bf16[2,8,32,128]{3,2,1,0:T(8,128)(2,1)S(1)} %get-tuple-element.8), channel_id=1, source_target_pairs={{0,1},{1,0},{2,3},{3,2},{4,5},{5,4},{6,7},{7,6},{8,9},{9,8},{10,11... | collective-permute-start | bytes 393224 | tf_op jit(solution)/shard_map/ppermute | solution.py:175
  7.2 1.0 %collective-permute-done = bf16[2,8,32,128]{3,2,1,0:T(8,128)(2,1)S(1)} collective-permute-done((bf16[2,8,32,128]{3,2,1,0:T(8,128)(2,1)S(1)}, bf16[2,8,32,128]{3,2,1,0:T(8,128)(2,1)S(1)}, u32[]{:S(2)}, u32[]{:S(2)}) %collective-permute-start) | collective-permute-done | bytes 131104 | tf_op jit(solution)/shard_map/ppermute | solution.py:175
  8.2 2.9 %collective-permute-start.1 = (bf16[1,8,32,128]{3,2,1,0:T(8,128)(2,1)S(1)}, bf16[1,8,32,128]{3,2,1,0:T(8,128)(2,1)S(1)}, u32[]{:S(2)}, u32[]{:S(2)}) collective-permute-start(bf16[1,8,32,128]{3,2,1,0:T(8,128)(2,1)S(1)} %slice.29), channel_id=1, source_target_pairs={{0,2},{1,3},{2,0},{3,1},{4,6},{5,7},{6,4},{7,5},{8,10},{9,11},{10,... | collective-permute-start | bytes 196616 | tf_op jit(solution)/shard_map/ppermute | solution.py:175
  11.2 2.4 %collective-permute-done.1 = bf16[1,8,32,128]{3,2,1,0:T(8,128)(2,1)S(1)} collective-permute-done((bf16[1,8,32,128]{3,2,1,0:T(8,128)(2,1)S(1)}, bf16[1,8,32,128]{3,2,1,0:T(8,128)(2,1)S(1)}, u32[]{:S(2)}, u32[]{:S(2)}) %collective-permute-start.1) | collective-permute-done | bytes 65568 | tf_op jit(solution)/shard_map/ppermute | solution.py:175
  13.6 3.0 %collective-permute-start.4 = (bf16[8,32,128]{2,1,0:T(8,128)(2,1)S(1)}, bf16[8,32,128]{2,1,0:T(8,128)(2,1)S(1)}, u32[]{:S(2)}, u32[]{:S(2)}) collective-permute-start(bf16[8,32,128]{2,1,0:T(8,128)(2,1)S(1)} %bitcast.10), channel_id=1, source_target_pairs={{0,16},{4,20},{8,24},{12,28},{16,0},{20,4},{24,8},{28,12},{1,17},{... | collective-permute-start | bytes 196616 | tf_op jit(solution)/shard_map/ppermute | solution.py:175
  16.6 2.3 %collective-permute-done.4.refs_4_ = bf16[8,32,128]{2,1,0:T(8,128)(2,1)S(1)} collective-permute-done((bf16[8,32,128]{2,1,0:T(8,128)(2,1)S(1)}, bf16[8,32,128]{2,1,0:T(8,128)(2,1)S(1)}, u32[]{:S(2)}, u32[]{:S(2)}) %collective-permute-start.4) | collective-permute-done | bytes 65568 | tf_op jit(solution)/shard_map/ppermute | solution.py:175
  18.9 2.8 %collective-permute-start.5 = (bf16[2,8,32,128]{3,2,1,0:T(8,128)(2,1)S(1)}, bf16[2,8,32,128]{3,2,1,0:T(8,128)(2,1)S(1)}, u32[]{:S(2)}, u32[]{:S(2)}) collective-permute-start(bf16[2,8,32,128]{3,2,1,0:T(8,128)(2,1)S(1)} %pad_maximum_fusion), channel_id=1, source_target_pairs={{0,12},{4,8},{8,4},{12,0},{16,28},{20,24},{24,20},{28,16},{1,13},{... | collective-permute-start | bytes 393224 | tf_op jit(solution)/shard_map/ppermute | solution.py:175
  21.8 0.0 copy-done
  21.8 0.2 place.1.place_ref
  22.0 0.5 %collective-permute-start.3 = (bf16[8,32,128]{2,1,0:T(8,128)(2,1)S(1)}, bf16[8,32,128]{2,1,0:T(8,128)(2,1)S(1)}, u32[]{:S(2)}, u32[]{:S(2)}) collective-permute-start(bf16[8,32,128]{2,1,0:T(8,128)(2,1)S(1)} %bitcast.11), channel_id=1, source_target_pairs={{0,8},{4,12},{8,0},{12,4},{16,24},{20,28},{24,16},{28,20},{1,9},{5... | collective-permute-start | bytes 196616 | tf_op jit(solution)/shard_map/ppermute | solution.py:175
  22.5 0.3 collective-permute-start.2
  22.8 1.8 %collective-permute-start.7 = (bf16[8,32,128]{2,1,0:T(8,128)(2,1)S(1)}, bf16[8,32,128]{2,1,0:T(8,128)(2,1)S(1)}, u32[]{:S(2)}, u32[]{:S(2)}) collective-permute-start(bf16[8,32,128]{2,1,0:T(8,128)(2,1)S(1)} %collective-permute-done.4.refs_4_), channel_id=1, source_target_pairs={{0,8},{4,12},{8,0},{12,4},{16,24},{20,28},{24,16},{28,20},{1,9},{5... | collective-permute-start | bytes 196616 | tf_op jit(solution)/shard_map/ppermute | solution.py:175
  24.6 1.5 %collective-permute-start.6 = (bf16[8,32,128]{2,1,0:T(8,128)(2,1)S(1)}, bf16[8,32,128]{2,1,0:T(8,128)(2,1)S(1)}, u32[]{:S(2)}, u32[]{:S(2)}) collective-permute-start(bf16[8,32,128]{2,1,0:T(8,128)(2,1)S(1)} %collective-permute-done.4.refs_4_), channel_id=1, source_target_pairs={{0,4},{4,0},{8,12},{12,8},{16,20},{20,16},{24,28},{28,24},{1,5},{5... | collective-permute-start | bytes 196616 | tf_op jit(solution)/shard_map/ppermute | solution.py:175
  26.1 0.0 collective-permute-done.5
  26.1 0.2 collective-permute-done.3.refs_2_
  26.3 0.5 %collective-permute-done.2.refs_1_ = bf16[8,32,128]{2,1,0:T(8,128)(2,1)S(1)} collective-permute-done((bf16[8,32,128]{2,1,0:T(8,128)(2,1)S(1)}, bf16[8,32,128]{2,1,0:T(8,128)(2,1)S(1)}, u32[]{:S(2)}, u32[]{:S(2)}) %collective-permute-start.2) | collective-permute-done | bytes 65568 | tf_op jit(solution)/shard_map/ppermute | solution.py:175
  26.8 0.3 collective-permute-done.7.refs_6_
  27.0 1.8 %collective-permute-done.6.refs_5_ = bf16[8,32,128]{2,1,0:T(8,128)(2,1)S(1)} collective-permute-done((bf16[8,32,128]{2,1,0:T(8,128)(2,1)S(1)}, bf16[8,32,128]{2,1,0:T(8,128)(2,1)S(1)}, u32[]{:S(2)}, u32[]{:S(2)}) %collective-permute-start.6) | collective-permute-done | bytes 65568 | tf_op jit(solution)/shard_map/ppermute | solution.py:175
  28.9 1.2 %correlate.1 = f32[4,2,32,256]{3,2,1,0:T(8,128)} custom-call(s32[1]{0:T(128)} %bitcast.me_ref, bf16[256,256]{1,0:T(8,128)(2,1)S(1)} %place.1.place_ref, bf16[8,32,128]{2,1,0:T(8,128)(2,1)S(1)} %bitcast.13, bf16[8,32,128]{2,1,0:T(8,128)(2,1)S(1)} %collective-permute-done.2.refs_1_, bf16[8,32,128]{2,1,0:T(8,128)(2,1)S(1)} %collective-permute-done.3.refs_2_, ...), custom_call_target="tpu_custom_call" | custom-call | tf_op jit(solution)/shard_map/correlate/pallas_call | solution.py:155
  (5 shorter events, 0.1 us)
Async XLA Ops:
  0.0 21.8 %copy-start = (s32[128]{0:T(128)S(1)}, s32[128]{0:T(128)}, u32[]{:S(2)}) copy-start(s32[128]{0:T(128)} %param.7) | copy-start | bytes 1540
  6.7 1.5 %collective-permute-start = (bf16[2,8,32,128]{3,2,1,0:T(8,128)(2,1)S(1)}, bf16[2,8,32,128]{3,2,1,0:T(8,128)(2,1)S(1)}, u32[]{:S(2)}, u32[]{:S(2)}) collective-permute-start(bf16[2,8,32,128]{3,2,1,0:T(8,128)(2,1)S(1)} %get-tuple-element.8), channel_id=1, source_target_pairs={{0,1},{1,0},{2,3},{3,2},{4,5},{5,4},{6,7},{7,6},{8,9},{9,8},{10,11... | collective-permute-start | bytes 393224 | tf_op jit(solution)/shard_map/ppermute | solution.py:175
  8.2 5.3 %collective-permute-start.1 = (bf16[1,8,32,128]{3,2,1,0:T(8,128)(2,1)S(1)}, bf16[1,8,32,128]{3,2,1,0:T(8,128)(2,1)S(1)}, u32[]{:S(2)}, u32[]{:S(2)}) collective-permute-start(bf16[1,8,32,128]{3,2,1,0:T(8,128)(2,1)S(1)} %slice.29), channel_id=1, source_target_pairs={{0,2},{1,3},{2,0},{3,1},{4,6},{5,7},{6,4},{7,5},{8,10},{9,11},{10,... | collective-permute-start | bytes 196616 | tf_op jit(solution)/shard_map/ppermute | solution.py:175
  13.6 5.3 %collective-permute-start.4 = (bf16[8,32,128]{2,1,0:T(8,128)(2,1)S(1)}, bf16[8,32,128]{2,1,0:T(8,128)(2,1)S(1)}, u32[]{:S(2)}, u32[]{:S(2)}) collective-permute-start(bf16[8,32,128]{2,1,0:T(8,128)(2,1)S(1)} %bitcast.10), channel_id=1, source_target_pairs={{0,16},{4,20},{8,24},{12,28},{16,0},{20,4},{24,8},{28,12},{1,17},{... | collective-permute-start | bytes 196616 | tf_op jit(solution)/shard_map/ppermute | solution.py:175
  18.9 7.2 %collective-permute-start.5 = (bf16[2,8,32,128]{3,2,1,0:T(8,128)(2,1)S(1)}, bf16[2,8,32,128]{3,2,1,0:T(8,128)(2,1)S(1)}, u32[]{:S(2)}, u32[]{:S(2)}) collective-permute-start(bf16[2,8,32,128]{3,2,1,0:T(8,128)(2,1)S(1)} %pad_maximum_fusion), channel_id=1, source_target_pairs={{0,12},{4,8},{8,4},{12,0},{16,28},{20,24},{24,20},{28,16},{1,13},{... | collective-permute-start | bytes 393224 | tf_op jit(solution)/shard_map/ppermute | solution.py:175
  22.0 4.3 %collective-permute-start.3 = (bf16[8,32,128]{2,1,0:T(8,128)(2,1)S(1)}, bf16[8,32,128]{2,1,0:T(8,128)(2,1)S(1)}, u32[]{:S(2)}, u32[]{:S(2)}) collective-permute-start(bf16[8,32,128]{2,1,0:T(8,128)(2,1)S(1)} %bitcast.11), channel_id=1, source_target_pairs={{0,8},{4,12},{8,0},{12,4},{16,24},{20,28},{24,16},{28,20},{1,9},{5... | collective-permute-start | bytes 196616 | tf_op jit(solution)/shard_map/ppermute | solution.py:175
  22.5 4.3 %collective-permute-start.2 = (bf16[8,32,128]{2,1,0:T(8,128)(2,1)S(1)}, bf16[8,32,128]{2,1,0:T(8,128)(2,1)S(1)}, u32[]{:S(2)}, u32[]{:S(2)}) collective-permute-start(bf16[8,32,128]{2,1,0:T(8,128)(2,1)S(1)} %bitcast.12), channel_id=1, source_target_pairs={{0,4},{4,0},{8,12},{12,8},{16,20},{20,16},{24,28},{28,24},{1,5},{5... | collective-permute-start | bytes 196616 | tf_op jit(solution)/shard_map/ppermute | solution.py:175
  22.8 4.3 %collective-permute-start.7 = (bf16[8,32,128]{2,1,0:T(8,128)(2,1)S(1)}, bf16[8,32,128]{2,1,0:T(8,128)(2,1)S(1)}, u32[]{:S(2)}, u32[]{:S(2)}) collective-permute-start(bf16[8,32,128]{2,1,0:T(8,128)(2,1)S(1)} %collective-permute-done.4.refs_4_), channel_id=1, source_target_pairs={{0,8},{4,12},{8,0},{12,4},{16,24},{20,28},{24,16},{28,20},{1,9},{5... | collective-permute-start | bytes 196616 | tf_op jit(solution)/shard_map/ppermute | solution.py:175
  24.6 4.3 %collective-permute-start.6 = (bf16[8,32,128]{2,1,0:T(8,128)(2,1)S(1)}, bf16[8,32,128]{2,1,0:T(8,128)(2,1)S(1)}, u32[]{:S(2)}, u32[]{:S(2)}) collective-permute-start(bf16[8,32,128]{2,1,0:T(8,128)(2,1)S(1)} %collective-permute-done.4.refs_4_), channel_id=1, source_target_pairs={{0,4},{4,0},{8,12},{12,8},{16,20},{20,16},{24,28},{28,24},{1,5},{5... | collective-permute-start | bytes 196616 | tf_op jit(solution)/shard_map/ppermute | solution.py:175

commit v3 on v2

--- a/solution.py
+++ b/solution.py
@@ -181,7 +181,8 @@
     total = keep + exchange(send, "tile", owners, 1).astype(F32)
     bit = 2
     while bit < owners:
-        sent = exchange(total[1::2].astype(BF16), "tile", owners, bit)
+        sent = total[1::2].astype(F32 if 2 * bit < owners else BF16)
+        sent = exchange(sent, "tile", owners, bit)
         total = total[0::2] + sent.astype(F32)
         bit *= 2
     own = total[0].astype(BF16)
@@ -197,12 +198,12 @@
 
 
 def solution(mesh):
-    groups = mesh.shape["sgroup"]
+    groups, owners = mesh.shape["sgroup"], mesh.shape["tile"]
     in_specs = (
         P(None, "sgroup", "tile", None, None, None),
         P(None, "sgroup", None, None, None),
         P("sgroup", "tile"),
         P(),
     )
-    run = functools.partial(body, groups, mesh.shape["tile"])
+    run = functools.partial(body, groups, owners)
     return jax.shard_map(run, mesh=mesh, in_specs=in_specs, out_specs=P("tile", None, "sgroup", None), check_vma=False)

time: 30.2 us -> 30.2 us (level)
  no operation moved by 1% of the time
where the time goes in v3:
time: 30.2 us; the launch traced here: 30.1 us
  starting transfers between devices  13.4 us (44%)
  waiting for transfers between devices  8.45 us (28%)
  Pallas kernels  8.03 us (27%)
    ppermute x8, starting transfers between devices, exchange(): return lax.ppermute(value, axis, [(i, i ^ bit) for i in range(size)])  13.4 us
    ppermute x8, waiting for transfers between devices, exchange(): return lax.ppermute(value, axis, [(i, i ^ bit) for i in range(size)])  8.45 us
    pallas_call x1, Pallas kernels, beam(): pl.pallas_call(functools.partial(beam_kernel, owners), out_shape=(jax.Sha...  6.64 us
    pallas_call x1, Pallas kernels, correlate(): pl.pallas_call(correlate_kernel, out_shape=jax.ShapeDtypeStruct(shape, F3...  1.21 us
  transfers between devices with their start and end apart: 8, of which 7 were waited for; matrix products, arithmetic and copies ran while one was open for 0% of the time, Pallas kernels for 1%

profile of v3, /device:TPU:0, one launch (start us, length us, event | category | flops | bytes accessed | tf_op | source)
XLA Modules:
  0.0 30.1 jit_solution(4667252760285127663)
XLA Ops:
  0.0 0.0 copy-start
  0.0 6.6 %beam.1 = (f32[2,8,32,128]{3,2,1,0:T(8,128)S(1)}, bf16[2,8,32,128]{3,2,1,0:T(8,128)(2,1)S(1)}) custom-call(s32[1]{0:T(128)} %bitcast.2.me_ref, s32[16,64]{1,0:T(8,128)} %index_hbm.1, bf16[2,16,2,16,256]{4,3,2,1,0:T(8,128)(2,1)} %bitcast.16, bf16[2,16,64,2,16,128]{5,4,3,2,1,0:T(8,128)(2,1)} %v_hbm.1), custom_call_target="tpu_custom_call" | custom-call | tf_op jit(solution)/shard_map/beam/pallas_call | solution.py:83
  6.7 0.6 %collective-permute-start = (bf16[2,8,32,128]{3,2,1,0:T(8,128)(2,1)S(1)}, bf16[2,8,32,128]{3,2,1,0:T(8,128)(2,1)S(1)}, u32[]{:S(2)}, u32[]{:S(2)}) collective-permute-start(bf16[2,8,32,128]{3,2,1,0:T(8,128)(2,1)S(1)} %get-tuple-element.8), channel_id=1, source_target_pairs={{0,1},{1,0},{2,3},{3,2},{4,5},{5,4},{6,7},{7,6},{8,9},{9,8},{10,11... | collective-permute-start | bytes 393224 | tf_op jit(solution)/shard_map/ppermute | solution.py:175
  7.2 1.0 %collective-permute-done = bf16[2,8,32,128]{3,2,1,0:T(8,128)(2,1)S(1)} collective-permute-done((bf16[2,8,32,128]{3,2,1,0:T(8,128)(2,1)S(1)}, bf16[2,8,32,128]{3,2,1,0:T(8,128)(2,1)S(1)}, u32[]{:S(2)}, u32[]{:S(2)}) %collective-permute-start) | collective-permute-done | bytes 131104 | tf_op jit(solution)/shard_map/ppermute | solution.py:175
  8.2 2.9 %collective-permute-start.1 = (bf16[1,8,32,128]{3,2,1,0:T(8,128)(2,1)S(1)}, bf16[1,8,32,128]{3,2,1,0:T(8,128)(2,1)S(1)}, u32[]{:S(2)}, u32[]{:S(2)}) collective-permute-start(bf16[1,8,32,128]{3,2,1,0:T(8,128)(2,1)S(1)} %slice.29), channel_id=1, source_target_pairs={{0,2},{1,3},{2,0},{3,1},{4,6},{5,7},{6,4},{7,5},{8,10},{9,11},{10,... | collective-permute-start | bytes 196616 | tf_op jit(solution)/shard_map/ppermute | solution.py:175
  11.2 2.4 %collective-permute-done.1 = bf16[1,8,32,128]{3,2,1,0:T(8,128)(2,1)S(1)} collective-permute-done((bf16[1,8,32,128]{3,2,1,0:T(8,128)(2,1)S(1)}, bf16[1,8,32,128]{3,2,1,0:T(8,128)(2,1)S(1)}, u32[]{:S(2)}, u32[]{:S(2)}) %collective-permute-start.1) | collective-permute-done | bytes 65568 | tf_op jit(solution)/shard_map/ppermute | solution.py:175
  13.6 3.0 %collective-permute-start.4 = (bf16[8,32,128]{2,1,0:T(8,128)(2,1)S(1)}, bf16[8,32,128]{2,1,0:T(8,128)(2,1)S(1)}, u32[]{:S(2)}, u32[]{:S(2)}) collective-permute-start(bf16[8,32,128]{2,1,0:T(8,128)(2,1)S(1)} %bitcast.10), channel_id=1, source_target_pairs={{0,16},{4,20},{8,24},{12,28},{16,0},{20,4},{24,8},{28,12},{1,17},{... | collective-permute-start | bytes 196616 | tf_op jit(solution)/shard_map/ppermute | solution.py:175
  16.6 2.3 %collective-permute-done.4.refs_4_ = bf16[8,32,128]{2,1,0:T(8,128)(2,1)S(1)} collective-permute-done((bf16[8,32,128]{2,1,0:T(8,128)(2,1)S(1)}, bf16[8,32,128]{2,1,0:T(8,128)(2,1)S(1)}, u32[]{:S(2)}, u32[]{:S(2)}) %collective-permute-start.4) | collective-permute-done | bytes 65568 | tf_op jit(solution)/shard_map/ppermute | solution.py:175
  18.9 2.8 %collective-permute-start.5 = (bf16[2,8,32,128]{3,2,1,0:T(8,128)(2,1)S(1)}, bf16[2,8,32,128]{3,2,1,0:T(8,128)(2,1)S(1)}, u32[]{:S(2)}, u32[]{:S(2)}) collective-permute-start(bf16[2,8,32,128]{3,2,1,0:T(8,128)(2,1)S(1)} %pad_maximum_fusion), channel_id=1, source_target_pairs={{0,12},{4,8},{8,4},{12,0},{16,28},{20,24},{24,20},{28,16},{1,13},{... | collective-permute-start | bytes 393224 | tf_op jit(solution)/shard_map/ppermute | solution.py:175
  21.8 0.0 copy-done
  21.8 0.2 place.1.place_ref
  22.0 0.5 %collective-permute-start.3 = (bf16[8,32,128]{2,1,0:T(8,128)(2,1)S(1)}, bf16[8,32,128]{2,1,0:T(8,128)(2,1)S(1)}, u32[]{:S(2)}, u32[]{:S(2)}) collective-permute-start(bf16[8,32,128]{2,1,0:T(8,128)(2,1)S(1)} %bitcast.11), channel_id=1, source_target_pairs={{0,8},{4,12},{8,0},{12,4},{16,24},{20,28},{24,16},{28,20},{1,9},{5... | collective-permute-start | bytes 196616 | tf_op jit(solution)/shard_map/ppermute | solution.py:175
  22.5 0.3 collective-permute-start.2
  22.8 1.8 %collective-permute-start.7 = (bf16[8,32,128]{2,1,0:T(8,128)(2,1)S(1)}, bf16[8,32,128]{2,1,0:T(8,128)(2,1)S(1)}, u32[]{:S(2)}, u32[]{:S(2)}) collective-permute-start(bf16[8,32,128]{2,1,0:T(8,128)(2,1)S(1)} %collective-permute-done.4.refs_4_), channel_id=1, source_target_pairs={{0,8},{4,12},{8,0},{12,4},{16,24},{20,28},{24,16},{28,20},{1,9},{5... | collective-permute-start | bytes 196616 | tf_op jit(solution)/shard_map/ppermute | solution.py:175
  24.6 1.5 %collective-permute-start.6 = (bf16[8,32,128]{2,1,0:T(8,128)(2,1)S(1)}, bf16[8,32,128]{2,1,0:T(8,128)(2,1)S(1)}, u32[]{:S(2)}, u32[]{:S(2)}) collective-permute-start(bf16[8,32,128]{2,1,0:T(8,128)(2,1)S(1)} %collective-permute-done.4.refs_4_), channel_id=1, source_target_pairs={{0,4},{4,0},{8,12},{12,8},{16,20},{20,16},{24,28},{28,24},{1,5},{5... | collective-permute-start | bytes 196616 | tf_op jit(solution)/shard_map/ppermute | solution.py:175
  26.1 0.0 collective-permute-done.5
  26.1 0.2 collective-permute-done.3.refs_2_
  26.3 0.5 %collective-permute-done.2.refs_1_ = bf16[8,32,128]{2,1,0:T(8,128)(2,1)S(1)} collective-permute-done((bf16[8,32,128]{2,1,0:T(8,128)(2,1)S(1)}, bf16[8,32,128]{2,1,0:T(8,128)(2,1)S(1)}, u32[]{:S(2)}, u32[]{:S(2)}) %collective-permute-start.2) | collective-permute-done | bytes 65568 | tf_op jit(solution)/shard_map/ppermute | solution.py:175
  26.8 0.3 collective-permute-done.7.refs_6_
  27.0 1.8 %collective-permute-done.6.refs_5_ = bf16[8,32,128]{2,1,0:T(8,128)(2,1)S(1)} collective-permute-done((bf16[8,32,128]{2,1,0:T(8,128)(2,1)S(1)}, bf16[8,32,128]{2,1,0:T(8,128)(2,1)S(1)}, u32[]{:S(2)}, u32[]{:S(2)}) %collective-permute-start.6) | collective-permute-done | bytes 65568 | tf_op jit(solution)/shard_map/ppermute | solution.py:175
  28.9 1.2 %correlate.1 = f32[4,2,32,256]{3,2,1,0:T(8,128)} custom-call(s32[1]{0:T(128)} %bitcast.me_ref, bf16[256,256]{1,0:T(8,128)(2,1)S(1)} %place.1.place_ref, bf16[8,32,128]{2,1,0:T(8,128)(2,1)S(1)} %bitcast.13, bf16[8,32,128]{2,1,0:T(8,128)(2,1)S(1)} %collective-permute-done.2.refs_1_, bf16[8,32,128]{2,1,0:T(8,128)(2,1)S(1)} %collective-permute-done.3.refs_2_, ...), custom_call_target="tpu_custom_call" | custom-call | tf_op jit(solution)/shard_map/correlate/pallas_call | solution.py:155
  (5 shorter events, 0.1 us)
Async XLA Ops:
  0.0 21.8 %copy-start = (s32[128]{0:T(128)S(1)}, s32[128]{0:T(128)}, u32[]{:S(2)}) copy-start(s32[128]{0:T(128)} %param.7) | copy-start | bytes 1540
  6.7 1.5 %collective-permute-start = (bf16[2,8,32,128]{3,2,1,0:T(8,128)(2,1)S(1)}, bf16[2,8,32,128]{3,2,1,0:T(8,128)(2,1)S(1)}, u32[]{:S(2)}, u32[]{:S(2)}) collective-permute-start(bf16[2,8,32,128]{3,2,1,0:T(8,128)(2,1)S(1)} %get-tuple-element.8), channel_id=1, source_target_pairs={{0,1},{1,0},{2,3},{3,2},{4,5},{5,4},{6,7},{7,6},{8,9},{9,8},{10,11... | collective-permute-start | bytes 393224 | tf_op jit(solution)/shard_map/ppermute | solution.py:175
  8.2 5.3 %collective-permute-start.1 = (bf16[1,8,32,128]{3,2,1,0:T(8,128)(2,1)S(1)}, bf16[1,8,32,128]{3,2,1,0:T(8,128)(2,1)S(1)}, u32[]{:S(2)}, u32[]{:S(2)}) collective-permute-start(bf16[1,8,32,128]{3,2,1,0:T(8,128)(2,1)S(1)} %slice.29), channel_id=1, source_target_pairs={{0,2},{1,3},{2,0},{3,1},{4,6},{5,7},{6,4},{7,5},{8,10},{9,11},{10,... | collective-permute-start | bytes 196616 | tf_op jit(solution)/shard_map/ppermute | solution.py:175
  13.6 5.3 %collective-permute-start.4 = (bf16[8,32,128]{2,1,0:T(8,128)(2,1)S(1)}, bf16[8,32,128]{2,1,0:T(8,128)(2,1)S(1)}, u32[]{:S(2)}, u32[]{:S(2)}) collective-permute-start(bf16[8,32,128]{2,1,0:T(8,128)(2,1)S(1)} %bitcast.10), channel_id=1, source_target_pairs={{0,16},{4,20},{8,24},{12,28},{16,0},{20,4},{24,8},{28,12},{1,17},{... | collective-permute-start | bytes 196616 | tf_op jit(solution)/shard_map/ppermute | solution.py:175
  18.9 7.2 %collective-permute-start.5 = (bf16[2,8,32,128]{3,2,1,0:T(8,128)(2,1)S(1)}, bf16[2,8,32,128]{3,2,1,0:T(8,128)(2,1)S(1)}, u32[]{:S(2)}, u32[]{:S(2)}) collective-permute-start(bf16[2,8,32,128]{3,2,1,0:T(8,128)(2,1)S(1)} %pad_maximum_fusion), channel_id=1, source_target_pairs={{0,12},{4,8},{8,4},{12,0},{16,28},{20,24},{24,20},{28,16},{1,13},{... | collective-permute-start | bytes 393224 | tf_op jit(solution)/shard_map/ppermute | solution.py:175
  22.0 4.3 %collective-permute-start.3 = (bf16[8,32,128]{2,1,0:T(8,128)(2,1)S(1)}, bf16[8,32,128]{2,1,0:T(8,128)(2,1)S(1)}, u32[]{:S(2)}, u32[]{:S(2)}) collective-permute-start(bf16[8,32,128]{2,1,0:T(8,128)(2,1)S(1)} %bitcast.11), channel_id=1, source_target_pairs={{0,8},{4,12},{8,0},{12,4},{16,24},{20,28},{24,16},{28,20},{1,9},{5... | collective-permute-start | bytes 196616 | tf_op jit(solution)/shard_map/ppermute | solution.py:175
  22.5 4.3 %collective-permute-start.2 = (bf16[8,32,128]{2,1,0:T(8,128)(2,1)S(1)}, bf16[8,32,128]{2,1,0:T(8,128)(2,1)S(1)}, u32[]{:S(2)}, u32[]{:S(2)}) collective-permute-start(bf16[8,32,128]{2,1,0:T(8,128)(2,1)S(1)} %bitcast.12), channel_id=1, source_target_pairs={{0,4},{4,0},{8,12},{12,8},{16,20},{20,16},{24,28},{28,24},{1,5},{5... | collective-permute-start | bytes 196616 | tf_op jit(solution)/shard_map/ppermute | solution.py:175
  22.8 4.3 %collective-permute-start.7 = (bf16[8,32,128]{2,1,0:T(8,128)(2,1)S(1)}, bf16[8,32,128]{2,1,0:T(8,128)(2,1)S(1)}, u32[]{:S(2)}, u32[]{:S(2)}) collective-permute-start(bf16[8,32,128]{2,1,0:T(8,128)(2,1)S(1)} %collective-permute-done.4.refs_4_), channel_id=1, source_target_pairs={{0,8},{4,12},{8,0},{12,4},{16,24},{20,28},{24,16},{28,20},{1,9},{5... | collective-permute-start | bytes 196616 | tf_op jit(solution)/shard_map/ppermute | solution.py:175
  24.6 4.3 %collective-permute-start.6 = (bf16[8,32,128]{2,1,0:T(8,128)(2,1)S(1)}, bf16[8,32,128]{2,1,0:T(8,128)(2,1)S(1)}, u32[]{:S(2)}, u32[]{:S(2)}) collective-permute-start(bf16[8,32,128]{2,1,0:T(8,128)(2,1)S(1)} %collective-permute-done.4.refs_4_), channel_id=1, source_target_pairs={{0,4},{4,0},{8,12},{12,8},{16,20},{20,16},{24,28},{28,24},{1,5},{5... | collective-permute-start | bytes 196616 | tf_op jit(solution)/shard_map/ppermute | solution.py:175

commit v4 on v3

--- a/solution.py
+++ b/solution.py
@@ -103,7 +103,9 @@
     total, stations = place_ref.shape[0], order_ref.shape[1]
     owns = jnp.where(order_ref[...] == iota((total, stations), 0) // polars, 1.0, 0.0).astype(BF16)
     column = iota((stations, total), 1)
-    slot = ((column // local) ^ me_ref[0]) * (local // polars) + (column % local) // polars
+    block, far = column // local, total // local // 2
+    block = jnp.where(block == far, far - 1, jnp.where(block == far - 1, far, block))
+    slot = (block ^ me_ref[0]) * (local // polars) + (column % local) // polars
     slots = jnp.where(iota((stations, total), 0) == slot, 1.0, 0.0).astype(BF16)
     same = iota((total, total), 0) % polars == iota((total, total), 1) % polars
     place_ref[...] = jnp.where(same, dot(owns, slots), 0.0).astype(BF16)
@@ -122,16 +124,41 @@
     )(me, order[None, :])
 
 
-def correlate_kernel(me_ref, place_ref, *refs):
+def both_parts(blocks, c, channels):
+    real = jnp.concatenate([b[c] for b in blocks], axis=0)
+    imag = jnp.concatenate([b[channels + c] for b in blocks], axis=0)
+    return jnp.concatenate([real, imag], axis=1)
+
+
+def early_kernel(place_ref, *refs):
+    blocks, row_ref = refs[:-1], refs[-1]
+    place = place_ref[:, : place_ref.shape[1] // 2]
+    channels = row_ref.shape[0]
+    for c in range(channels):
+        row_ref[c] = dot(place, both_parts(blocks, c, channels)).astype(BF16)
+
+
+def early(place, blocks):
+    inner, _, spectra = blocks[0].shape
+    vmem = pl.BlockSpec(memory_space=pltpu.VMEM)
+    return pl.pallas_call(
+        early_kernel,
+        out_shape=jax.ShapeDtypeStruct((inner // 2, place.shape[0], 2 * spectra), BF16),
+        in_specs=[vmem] * (1 + len(blocks)),
+        out_specs=vmem,
+        compiler_params=pltpu.CompilerParams(vmem_limit_bytes=48 << 20),
+        name="early",
+    )(place, *blocks)
+
+
+def correlate_kernel(me_ref, place_ref, early_ref, *refs):
     blocks, (out_hbm, row_ref, out_ref, sem) = refs[:-4], refs[-4:]
     inner, local, spectra = blocks[0].shape
     channels = inner // 2
-    me, place = me_ref[0], place_ref[...]
+    me, place = me_ref[0], place_ref[:, place_ref.shape[1] // 2 :]
     scale = 1.0 / spectra
     for c in range(channels):
-        real = jnp.concatenate([b[c] for b in blocks], axis=0)
-        imag = jnp.concatenate([b[channels + c] for b in blocks], axis=0)
-        row_ref[c] = dot(place, jnp.concatenate([real, imag], axis=1)).astype(BF16)
+        row_ref[c] = dot(place, both_parts(blocks, c, channels)).astype(BF16) + early_ref[c]
     rows, copies = pl.ds(pl.multiple_of(me * local, local), local), []
     for c in range(channels):
         mine = row_ref[c, rows, :]
@@ -147,15 +174,15 @@
         copy.wait()
 
 
-def correlate(me, place, blocks):
+def correlate(me, place, ordered, blocks):
     inner, local, spectra = blocks[0].shape
-    total = len(blocks) * local
+    total = place.shape[0]
     shape = (inner // 2, 2, local, total)
     vmem = pl.BlockSpec(memory_space=pltpu.VMEM)
     return pl.pallas_call(
         correlate_kernel,
         out_shape=jax.ShapeDtypeStruct(shape, F32),
-        in_specs=[pl.BlockSpec(memory_space=pltpu.SMEM), vmem] + [vmem] * len(blocks),
+        in_specs=[pl.BlockSpec(memory_space=pltpu.SMEM)] + [vmem] * (2 + len(blocks)),
         out_specs=pl.BlockSpec(memory_space=pltpu.HBM),
         scratch_shapes=[
             pltpu.VMEM((inner // 2, total, 2 * spectra), BF16),
@@ -164,7 +191,7 @@
         ],
         compiler_params=pltpu.CompilerParams(vmem_limit_bytes=48 << 20),
         name="correlate",
-    )(me, place, *blocks)
+    )(me, place, ordered, *blocks)
 
 
 def body(groups, owners, voltages, weights, antenna_slot_index, station_order):
@@ -194,7 +221,9 @@
     for i in range(1, far - 1):
         blocks[far + i] = share(blocks[far], i)
     place = placement(group[None], station_order, voltages.shape[3], own.shape[1])
-    return correlate(group[None], place, [blocks[i] for i in range(groups)])
+    first = [*range(far - 1), far]
+    ordered = early(place, [blocks[i] for i in first])
+    return correlate(group[None], place, ordered, [blocks[i] for i in range(groups) if i not in first])
 
 
 def solution(mesh):

time: 30.2 us -> 30.2 us (level)
  transfers between devices with their start and end apart: 8 -> 8, of which waited for: 7 -> 6; matrix products, arithmetic and copies ran while one was open for 0% -> 0% of each run, Pallas kernels for 1% -> 2%
where the time goes in v4:
time: 30.2 us; the launch traced here: 30 us
  starting transfers between devices  13.4 us (44%)
  Pallas kernels  8.29 us (27%)
  waiting for transfers between devices  8.15 us (27%)
    ppermute x8, starting transfers between devices, exchange(): return lax.ppermute(value, axis, [(i, i ^ bit) for i in range(size)])  13.4 us
    ppermute x8, waiting for transfers between devices, exchange(): return lax.ppermute(value, axis, [(i, i ^ bit) for i in range(size)])  8.15 us
    pallas_call x1, Pallas kernels, beam(): pl.pallas_call(functools.partial(beam_kernel, owners), out_shape=(jax.Sha...  6.64 us
    pallas_call x1, Pallas kernels, correlate(): pl.pallas_call(correlate_kernel, out_shape=jax.ShapeDtypeStruct(shape, F3...  1.19 us
  transfers between devices with their start and end apart: 8, of which 6 were waited for; matrix products, arithmetic and copies ran while one was open for 0% of the time, Pallas kernels for 2%

profile of v4, /device:TPU:0, one launch (start us, length us, event | category | flops | bytes accessed | tf_op | source)
XLA Modules:
  0.0 30.0 jit_solution(2169916722170674662)
XLA Ops:
  0.0 0.0 copy-start
  0.0 6.6 %beam.1 = (f32[2,8,32,128]{3,2,1,0:T(8,128)S(1)}, bf16[2,8,32,128]{3,2,1,0:T(8,128)(2,1)S(1)}) custom-call(s32[1]{0:T(128)} %bitcast.2.me_ref, s32[16,64]{1,0:T(8,128)} %index_hbm.1, bf16[2,16,2,16,256]{4,3,2,1,0:T(8,128)(2,1)} %bitcast.16, bf16[2,16,64,2,16,128]{5,4,3,2,1,0:T(8,128)(2,1)} %v_hbm.1), custom_call_target="tpu_custom_call" | custom-call | tf_op jit(solution)/shard_map/beam/pallas_call | solution.py:83
  6.7 0.6 %collective-permute-start = (bf16[2,8,32,128]{3,2,1,0:T(8,128)(2,1)S(1)}, bf16[2,8,32,128]{3,2,1,0:T(8,128)(2,1)S(1)}, u32[]{:S(2)}, u32[]{:S(2)}) collective-permute-start(bf16[2,8,32,128]{3,2,1,0:T(8,128)(2,1)S(1)} %get-tuple-element.8), channel_id=1, source_target_pairs={{0,1},{1,0},{2,3},{3,2},{4,5},{5,4},{6,7},{7,6},{8,9},{9,8},{10,11... | collective-permute-start | bytes 393224 | tf_op jit(solution)/shard_map/ppermute | solution.py:202
  7.2 1.0 %collective-permute-done = bf16[2,8,32,128]{3,2,1,0:T(8,128)(2,1)S(1)} collective-permute-done((bf16[2,8,32,128]{3,2,1,0:T(8,128)(2,1)S(1)}, bf16[2,8,32,128]{3,2,1,0:T(8,128)(2,1)S(1)}, u32[]{:S(2)}, u32[]{:S(2)}) %collective-permute-start) | collective-permute-done | bytes 131104 | tf_op jit(solution)/shard_map/ppermute | solution.py:202
  8.2 2.9 %collective-permute-start.1 = (bf16[1,8,32,128]{3,2,1,0:T(8,128)(2,1)S(1)}, bf16[1,8,32,128]{3,2,1,0:T(8,128)(2,1)S(1)}, u32[]{:S(2)}, u32[]{:S(2)}) collective-permute-start(bf16[1,8,32,128]{3,2,1,0:T(8,128)(2,1)S(1)} %slice.29), channel_id=1, source_target_pairs={{0,2},{1,3},{2,0},{3,1},{4,6},{5,7},{6,4},{7,5},{8,10},{9,11},{10,... | collective-permute-start | bytes 196616 | tf_op jit(solution)/shard_map/ppermute | solution.py:202
  11.2 2.4 %collective-permute-done.1 = bf16[1,8,32,128]{3,2,1,0:T(8,128)(2,1)S(1)} collective-permute-done((bf16[1,8,32,128]{3,2,1,0:T(8,128)(2,1)S(1)}, bf16[1,8,32,128]{3,2,1,0:T(8,128)(2,1)S(1)}, u32[]{:S(2)}, u32[]{:S(2)}) %collective-permute-start.1) | collective-permute-done | bytes 65568 | tf_op jit(solution)/shard_map/ppermute | solution.py:202
  13.6 3.0 %collective-permute-start.4 = (bf16[8,32,128]{2,1,0:T(8,128)(2,1)S(1)}, bf16[8,32,128]{2,1,0:T(8,128)(2,1)S(1)}, u32[]{:S(2)}, u32[]{:S(2)}) collective-permute-start(bf16[8,32,128]{2,1,0:T(8,128)(2,1)S(1)} %bitcast.10), channel_id=1, source_target_pairs={{0,16},{4,20},{8,24},{12,28},{16,0},{20,4},{24,8},{28,12},{1,17},{... | collective-permute-start | bytes 196616 | tf_op jit(solution)/shard_map/ppermute | solution.py:202
  16.6 2.3 %collective-permute-done.4.refs_3_ = bf16[8,32,128]{2,1,0:T(8,128)(2,1)S(1)} collective-permute-done((bf16[8,32,128]{2,1,0:T(8,128)(2,1)S(1)}, bf16[8,32,128]{2,1,0:T(8,128)(2,1)S(1)}, u32[]{:S(2)}, u32[]{:S(2)}) %collective-permute-start.4) | collective-permute-done | bytes 65568 | tf_op jit(solution)/shard_map/ppermute | solution.py:202
  18.9 2.8 %collective-permute-start.5 = (bf16[2,8,32,128]{3,2,1,0:T(8,128)(2,1)S(1)}, bf16[2,8,32,128]{3,2,1,0:T(8,128)(2,1)S(1)}, u32[]{:S(2)}, u32[]{:S(2)}) collective-permute-start(bf16[2,8,32,128]{3,2,1,0:T(8,128)(2,1)S(1)} %pad_maximum_fusion), channel_id=1, source_target_pairs={{0,12},{4,8},{8,4},{12,0},{16,28},{20,24},{24,20},{28,16},{1,13},{... | collective-permute-start | bytes 393224 | tf_op jit(solution)/shard_map/ppermute | solution.py:202
  21.8 0.5 %collective-permute-start.3 = (bf16[8,32,128]{2,1,0:T(8,128)(2,1)S(1)}, bf16[8,32,128]{2,1,0:T(8,128)(2,1)S(1)}, u32[]{:S(2)}, u32[]{:S(2)}) collective-permute-start(bf16[8,32,128]{2,1,0:T(8,128)(2,1)S(1)} %bitcast.11), channel_id=1, source_target_pairs={{0,8},{4,12},{8,0},{12,4},{16,24},{20,28},{24,16},{28,20},{1,9},{5... | collective-permute-start | bytes 196616 | tf_op jit(solution)/shard_map/ppermute | solution.py:202
  22.2 0.3 collective-permute-start.2
  22.5 0.0 copy-done
  22.5 0.2 place.1.place_ref
  22.7 1.9 %collective-permute-start.7 = (bf16[8,32,128]{2,1,0:T(8,128)(2,1)S(1)}, bf16[8,32,128]{2,1,0:T(8,128)(2,1)S(1)}, u32[]{:S(2)}, u32[]{:S(2)}) collective-permute-start(bf16[8,32,128]{2,1,0:T(8,128)(2,1)S(1)} %collective-permute-done.4.refs_3_), channel_id=1, source_target_pairs={{0,8},{4,12},{8,0},{12,4},{16,24},{20,28},{24,16},{28,20},{1,9},{5... | collective-permute-start | bytes 196616 | tf_op jit(solution)/shard_map/ppermute | solution.py:202
  24.6 1.5 %collective-permute-start.6 = (bf16[8,32,128]{2,1,0:T(8,128)(2,1)S(1)}, bf16[8,32,128]{2,1,0:T(8,128)(2,1)S(1)}, u32[]{:S(2)}, u32[]{:S(2)}) collective-permute-start(bf16[8,32,128]{2,1,0:T(8,128)(2,1)S(1)} %collective-permute-done.4.refs_3_), channel_id=1, source_target_pairs={{0,4},{4,0},{8,12},{12,8},{16,20},{20,16},{24,28},{28,24},{1,5},{5... | collective-permute-start | bytes 196616 | tf_op jit(solution)/shard_map/ppermute | solution.py:202
  26.1 0.0 collective-permute-done.3.refs_2_
  26.1 0.4 %collective-permute-done.2.refs_1_ = bf16[8,32,128]{2,1,0:T(8,128)(2,1)S(1)} collective-permute-done((bf16[8,32,128]{2,1,0:T(8,128)(2,1)S(1)}, bf16[8,32,128]{2,1,0:T(8,128)(2,1)S(1)}, u32[]{:S(2)}, u32[]{:S(2)}) %collective-permute-start.2) | collective-permute-done | bytes 65568 | tf_op jit(solution)/shard_map/ppermute | solution.py:202
  26.5 0.3 early.1.early_ref
  26.8 0.0 collective-permute-done.5
  26.8 0.2 collective-permute-done.7.refs_2_
  27.0 1.8 %collective-permute-done.6.refs_1_ = bf16[8,32,128]{2,1,0:T(8,128)(2,1)S(1)} collective-permute-done((bf16[8,32,128]{2,1,0:T(8,128)(2,1)S(1)}, bf16[8,32,128]{2,1,0:T(8,128)(2,1)S(1)}, u32[]{:S(2)}, u32[]{:S(2)}) %collective-permute-start.6) | collective-permute-done | bytes 65568 | tf_op jit(solution)/shard_map/ppermute | solution.py:202
  28.9 1.2 %correlate.1 = f32[4,2,32,256]{3,2,1,0:T(8,128)} custom-call(s32[1]{0:T(128)} %bitcast.me_ref, bf16[256,256]{1,0:T(8,128)(2,1)S(1)} %place.1.place_ref, bf16[4,256,256]{2,1,0:T(8,128)(2,1)S(1)} %early.1.early_ref, bf16[8,32,128]{2,1,0:T(8,128)(2,1)S(1)} %get-tuple-element.10.refs_0_, bf16[8,32,128]{2,1,0:T(8,128)(2,1)S(1)} %collective-permute-done.6.refs_1_, ...), custom_call_target="tpu_custom_call" | custom-call | tf_op jit(solution)/shard_map/correlate/pallas_call | solution.py:182
  (5 shorter events, 0.1 us)
Async XLA Ops:
  0.0 22.5 %copy-start = (s32[128]{0:T(128)S(1)}, s32[128]{0:T(128)}, u32[]{:S(2)}) copy-start(s32[128]{0:T(128)} %param.7) | copy-start | bytes 1540
  6.7 1.5 %collective-permute-start = (bf16[2,8,32,128]{3,2,1,0:T(8,128)(2,1)S(1)}, bf16[2,8,32,128]{3,2,1,0:T(8,128)(2,1)S(1)}, u32[]{:S(2)}, u32[]{:S(2)}) collective-permute-start(bf16[2,8,32,128]{3,2,1,0:T(8,128)(2,1)S(1)} %get-tuple-element.8), channel_id=1, source_target_pairs={{0,1},{1,0},{2,3},{3,2},{4,5},{5,4},{6,7},{7,6},{8,9},{9,8},{10,11... | collective-permute-start | bytes 393224 | tf_op jit(solution)/shard_map/ppermute | solution.py:202
  8.2 5.3 %collective-permute-start.1 = (bf16[1,8,32,128]{3,2,1,0:T(8,128)(2,1)S(1)}, bf16[1,8,32,128]{3,2,1,0:T(8,128)(2,1)S(1)}, u32[]{:S(2)}, u32[]{:S(2)}) collective-permute-start(bf16[1,8,32,128]{3,2,1,0:T(8,128)(2,1)S(1)} %slice.29), channel_id=1, source_target_pairs={{0,2},{1,3},{2,0},{3,1},{4,6},{5,7},{6,4},{7,5},{8,10},{9,11},{10,... | collective-permute-start | bytes 196616 | tf_op jit(solution)/shard_map/ppermute | solution.py:202
  13.6 5.3 %collective-permute-start.4 = (bf16[8,32,128]{2,1,0:T(8,128)(2,1)S(1)}, bf16[8,32,128]{2,1,0:T(8,128)(2,1)S(1)}, u32[]{:S(2)}, u32[]{:S(2)}) collective-permute-start(bf16[8,32,128]{2,1,0:T(8,128)(2,1)S(1)} %bitcast.10), channel_id=1, source_target_pairs={{0,16},{4,20},{8,24},{12,28},{16,0},{20,4},{24,8},{28,12},{1,17},{... | collective-permute-start | bytes 196616 | tf_op jit(solution)/shard_map/ppermute | solution.py:202
  18.9 7.9 %collective-permute-start.5 = (bf16[2,8,32,128]{3,2,1,0:T(8,128)(2,1)S(1)}, bf16[2,8,32,128]{3,2,1,0:T(8,128)(2,1)S(1)}, u32[]{:S(2)}, u32[]{:S(2)}) collective-permute-start(bf16[2,8,32,128]{3,2,1,0:T(8,128)(2,1)S(1)} %pad_maximum_fusion), channel_id=1, source_target_pairs={{0,12},{4,8},{8,4},{12,0},{16,28},{20,24},{24,20},{28,16},{1,13},{... | collective-permute-start | bytes 393224 | tf_op jit(solution)/shard_map/ppermute | solution.py:202
  21.8 4.3 %collective-permute-start.3 = (bf16[8,32,128]{2,1,0:T(8,128)(2,1)S(1)}, bf16[8,32,128]{2,1,0:T(8,128)(2,1)S(1)}, u32[]{:S(2)}, u32[]{:S(2)}) collective-permute-start(bf16[8,32,128]{2,1,0:T(8,128)(2,1)S(1)} %bitcast.11), channel_id=1, source_target_pairs={{0,8},{4,12},{8,0},{12,4},{16,24},{20,28},{24,16},{28,20},{1,9},{5... | collective-permute-start | bytes 196616 | tf_op jit(solution)/shard_map/ppermute | solution.py:202
  22.2 4.3 %collective-permute-start.2 = (bf16[8,32,128]{2,1,0:T(8,128)(2,1)S(1)}, bf16[8,32,128]{2,1,0:T(8,128)(2,1)S(1)}, u32[]{:S(2)}, u32[]{:S(2)}) collective-permute-start(bf16[8,32,128]{2,1,0:T(8,128)(2,1)S(1)} %bitcast.12), channel_id=1, source_target_pairs={{0,4},{4,0},{8,12},{12,8},{16,20},{20,16},{24,28},{28,24},{1,5},{5... | collective-permute-start | bytes 196616 | tf_op jit(solution)/shard_map/ppermute | solution.py:202
  22.7 4.3 %collective-permute-start.7 = (bf16[8,32,128]{2,1,0:T(8,128)(2,1)S(1)}, bf16[8,32,128]{2,1,0:T(8,128)(2,1)S(1)}, u32[]{:S(2)}, u32[]{:S(2)}) collective-permute-start(bf16[8,32,128]{2,1,0:T(8,128)(2,1)S(1)} %collective-permute-done.4.refs_3_), channel_id=1, source_target_pairs={{0,8},{4,12},{8,0},{12,4},{16,24},{20,28},{24,16},{28,20},{1,9},{5... | collective-permute-start | bytes 196616 | tf_op jit(solution)/shard_map/ppermute | solution.py:202
  24.6 4.3 %collective-permute-start.6 = (bf16[8,32,128]{2,1,0:T(8,128)(2,1)S(1)}, bf16[8,32,128]{2,1,0:T(8,128)(2,1)S(1)}, u32[]{:S(2)}, u32[]{:S(2)}) collective-permute-start(bf16[8,32,128]{2,1,0:T(8,128)(2,1)S(1)} %collective-permute-done.4.refs_3_), channel_id=1, source_target_pairs={{0,4},{4,0},{8,12},{12,8},{16,20},{20,16},{24,28},{28,24},{1,5},{5... | collective-permute-start | bytes 196616 | tf_op jit(solution)/shard_map/ppermute | solution.py:202

commit v5 on v4

--- a/solution.py
+++ b/solution.py
@@ -205,13 +205,14 @@
         return exchange(value, "sgroup", groups, bit)
 
     keep, send = beam(owners, tile[None], antenna_slot_index, jnp.transpose(weights, (0, 1, 3, 4, 2)), voltages)
-    total = keep + exchange(send, "tile", owners, 1).astype(F32)
+    halves = [keep, exchange(send, "tile", owners, 1)]
     bit = 2
     while bit < owners:
-        sent = total[1::2].astype(F32 if 2 * bit < owners else BF16)
+        sent = sum(h[1::2].astype(F32) for h in halves).astype(F32 if 2 * bit < owners else BF16)
         sent = exchange(sent, "tile", owners, bit)
-        total = total[0::2] + sent.astype(F32)
+        halves = [h[0::2] for h in halves] + [sent]
         bit *= 2
+    total = sum(h.astype(F32) for h in halves)
     own = total[0].astype(BF16)
     blocks = {0: own, far: share(own, far)}
     for i in range(far - 2, 0, -1):

time: 30.2 us -> 30.2 us (level)
  no operation moved by 1% of the time
where the time goes in v5:
time: 30.2 us; the launch traced here: 30 us
  starting transfers between devices  13.4 us (44%)
  Pallas kernels  8.29 us (27%)
  waiting for transfers between devices  8.15 us (27%)
    ppermute x8, starting transfers between devices, exchange(): return lax.ppermute(value, axis, [(i, i ^ bit) for i in range(size)])  13.4 us
    ppermute x8, waiting for transfers between devices, exchange(): return lax.ppermute(value, axis, [(i, i ^ bit) for i in range(size)])  8.15 us
    pallas_call x1, Pallas kernels, beam(): pl.pallas_call(functools.partial(beam_kernel, owners), out_shape=(jax.Sha...  6.64 us
    pallas_call x1, Pallas kernels, correlate(): pl.pallas_call(correlate_kernel, out_shape=jax.ShapeDtypeStruct(shape, F3...  1.2 us
  transfers between devices with their start and end apart: 8, of which 6 were waited for; matrix products, arithmetic and copies ran while one was open for 0% of the time, Pallas kernels for 2%

profile of v5, /device:TPU:0, one launch (start us, length us, event | category | flops | bytes accessed | tf_op | source)
XLA Modules:
  0.0 30.0 jit_solution(16957698075409252229)
XLA Ops:
  0.0 0.0 copy-start
  0.0 6.6 %beam.1 = (f32[2,8,32,128]{3,2,1,0:T(8,128)S(1)}, bf16[2,8,32,128]{3,2,1,0:T(8,128)(2,1)S(1)}) custom-call(s32[1]{0:T(128)} %bitcast.2.me_ref, s32[16,64]{1,0:T(8,128)} %index_hbm.1, bf16[2,16,2,16,256]{4,3,2,1,0:T(8,128)(2,1)} %bitcast.16, bf16[2,16,64,2,16,128]{5,4,3,2,1,0:T(8,128)(2,1)} %v_hbm.1), custom_call_target="tpu_custom_call" | custom-call | tf_op jit(solution)/shard_map/beam/pallas_call | solution.py:83
  6.7 0.6 %collective-permute-start = (bf16[2,8,32,128]{3,2,1,0:T(8,128)(2,1)S(1)}, bf16[2,8,32,128]{3,2,1,0:T(8,128)(2,1)S(1)}, u32[]{:S(2)}, u32[]{:S(2)}) collective-permute-start(bf16[2,8,32,128]{3,2,1,0:T(8,128)(2,1)S(1)} %get-tuple-element.8), channel_id=1, source_target_pairs={{0,1},{1,0},{2,3},{3,2},{4,5},{5,4},{6,7},{7,6},{8,9},{9,8},{10,11... | collective-permute-start | bytes 393224 | tf_op jit(solution)/shard_map/ppermute | solution.py:202
  7.2 1.0 %collective-permute-done = bf16[2,8,32,128]{3,2,1,0:T(8,128)(2,1)S(1)} collective-permute-done((bf16[2,8,32,128]{3,2,1,0:T(8,128)(2,1)S(1)}, bf16[2,8,32,128]{3,2,1,0:T(8,128)(2,1)S(1)}, u32[]{:S(2)}, u32[]{:S(2)}) %collective-permute-start) | collective-permute-done | bytes 131104 | tf_op jit(solution)/shard_map/ppermute | solution.py:202
  8.2 2.9 %collective-permute-start.1 = (bf16[1,8,32,128]{3,2,1,0:T(8,128)(2,1)S(1)}, bf16[1,8,32,128]{3,2,1,0:T(8,128)(2,1)S(1)}, u32[]{:S(2)}, u32[]{:S(2)}) collective-permute-start(bf16[1,8,32,128]{3,2,1,0:T(8,128)(2,1)S(1)} %add_convert_fusion.1), channel_id=1, source_target_pairs={{0,2},{1,3},{2,0},{3,1},{4,6},{5,7},{6,4},{7,5},{8,10},{9,11},{10,... | collective-permute-start | bytes 196616 | tf_op jit(solution)/shard_map/ppermute | solution.py:202
  11.1 2.4 %collective-permute-done.1 = bf16[1,8,32,128]{3,2,1,0:T(8,128)(2,1)S(1)} collective-permute-done((bf16[1,8,32,128]{3,2,1,0:T(8,128)(2,1)S(1)}, bf16[1,8,32,128]{3,2,1,0:T(8,128)(2,1)S(1)}, u32[]{:S(2)}, u32[]{:S(2)}) %collective-permute-start.1) | collective-permute-done | bytes 65568 | tf_op jit(solution)/shard_map/ppermute | solution.py:202
  13.6 3.0 %collective-permute-start.4 = (bf16[8,32,128]{2,1,0:T(8,128)(2,1)S(1)}, bf16[8,32,128]{2,1,0:T(8,128)(2,1)S(1)}, u32[]{:S(2)}, u32[]{:S(2)}) collective-permute-start(bf16[8,32,128]{2,1,0:T(8,128)(2,1)S(1)} %bitcast.10), channel_id=1, source_target_pairs={{0,16},{4,20},{8,24},{12,28},{16,0},{20,4},{24,8},{28,12},{1,17},{... | collective-permute-start | bytes 196616 | tf_op jit(solution)/shard_map/ppermute | solution.py:202
  16.6 2.3 %collective-permute-done.4.refs_3_ = bf16[8,32,128]{2,1,0:T(8,128)(2,1)S(1)} collective-permute-done((bf16[8,32,128]{2,1,0:T(8,128)(2,1)S(1)}, bf16[8,32,128]{2,1,0:T(8,128)(2,1)S(1)}, u32[]{:S(2)}, u32[]{:S(2)}) %collective-permute-start.4) | collective-permute-done | bytes 65568 | tf_op jit(solution)/shard_map/ppermute | solution.py:202
  18.9 2.8 %collective-permute-start.5 = (bf16[2,8,32,128]{3,2,1,0:T(8,128)(2,1)S(1)}, bf16[2,8,32,128]{3,2,1,0:T(8,128)(2,1)S(1)}, u32[]{:S(2)}, u32[]{:S(2)}) collective-permute-start(bf16[2,8,32,128]{3,2,1,0:T(8,128)(2,1)S(1)} %pad_maximum_fusion), channel_id=1, source_target_pairs={{0,12},{4,8},{8,4},{12,0},{16,28},{20,24},{24,20},{28,16},{1,13},{... | collective-permute-start | bytes 393224 | tf_op jit(solution)/shard_map/ppermute | solution.py:202
  21.8 0.5 %collective-permute-start.3 = (bf16[8,32,128]{2,1,0:T(8,128)(2,1)S(1)}, bf16[8,32,128]{2,1,0:T(8,128)(2,1)S(1)}, u32[]{:S(2)}, u32[]{:S(2)}) collective-permute-start(bf16[8,32,128]{2,1,0:T(8,128)(2,1)S(1)} %bitcast.11), channel_id=1, source_target_pairs={{0,8},{4,12},{8,0},{12,4},{16,24},{20,28},{24,16},{28,20},{1,9},{5... | collective-permute-start | bytes 196616 | tf_op jit(solution)/shard_map/ppermute | solution.py:202
  22.2 0.3 collective-permute-start.2
  22.5 0.0 copy-done
  22.5 0.2 place.1.place_ref
  22.7 1.9 %collective-permute-start.7 = (bf16[8,32,128]{2,1,0:T(8,128)(2,1)S(1)}, bf16[8,32,128]{2,1,0:T(8,128)(2,1)S(1)}, u32[]{:S(2)}, u32[]{:S(2)}) collective-permute-start(bf16[8,32,128]{2,1,0:T(8,128)(2,1)S(1)} %collective-permute-done.4.refs_3_), channel_id=1, source_target_pairs={{0,8},{4,12},{8,0},{12,4},{16,24},{20,28},{24,16},{28,20},{1,9},{5... | collective-permute-start | bytes 196616 | tf_op jit(solution)/shard_map/ppermute | solution.py:202
  24.6 1.5 %collective-permute-start.6 = (bf16[8,32,128]{2,1,0:T(8,128)(2,1)S(1)}, bf16[8,32,128]{2,1,0:T(8,128)(2,1)S(1)}, u32[]{:S(2)}, u32[]{:S(2)}) collective-permute-start(bf16[8,32,128]{2,1,0:T(8,128)(2,1)S(1)} %collective-permute-done.4.refs_3_), channel_id=1, source_target_pairs={{0,4},{4,0},{8,12},{12,8},{16,20},{20,16},{24,28},{28,24},{1,5},{5... | collective-permute-start | bytes 196616 | tf_op jit(solution)/shard_map/ppermute | solution.py:202
  26.1 0.0 collective-permute-done.3.refs_2_
  26.1 0.4 %collective-permute-done.2.refs_1_ = bf16[8,32,128]{2,1,0:T(8,128)(2,1)S(1)} collective-permute-done((bf16[8,32,128]{2,1,0:T(8,128)(2,1)S(1)}, bf16[8,32,128]{2,1,0:T(8,128)(2,1)S(1)}, u32[]{:S(2)}, u32[]{:S(2)}) %collective-permute-start.2) | collective-permute-done | bytes 65568 | tf_op jit(solution)/shard_map/ppermute | solution.py:202
  26.5 0.3 early.1.early_ref
  26.8 0.0 collective-permute-done.5
  26.8 0.2 collective-permute-done.7.refs_2_
  27.0 1.8 %collective-permute-done.6.refs_1_ = bf16[8,32,128]{2,1,0:T(8,128)(2,1)S(1)} collective-permute-done((bf16[8,32,128]{2,1,0:T(8,128)(2,1)S(1)}, bf16[8,32,128]{2,1,0:T(8,128)(2,1)S(1)}, u32[]{:S(2)}, u32[]{:S(2)}) %collective-permute-start.6) | collective-permute-done | bytes 65568 | tf_op jit(solution)/shard_map/ppermute | solution.py:202
  28.8 1.2 %correlate.1 = f32[4,2,32,256]{3,2,1,0:T(8,128)} custom-call(s32[1]{0:T(128)} %bitcast.me_ref, bf16[256,256]{1,0:T(8,128)(2,1)S(1)} %place.1.place_ref, bf16[4,256,256]{2,1,0:T(8,128)(2,1)S(1)} %early.1.early_ref, bf16[8,32,128]{2,1,0:T(8,128)(2,1)S(1)} %get-tuple-element.10.refs_0_, bf16[8,32,128]{2,1,0:T(8,128)(2,1)S(1)} %collective-permute-done.6.refs_1_, ...), custom_call_target="tpu_custom_call" | custom-call | tf_op jit(solution)/shard_map/correlate/pallas_call | solution.py:182
  (4 shorter events, 0.1 us)
Async XLA Ops:
  0.0 22.5 %copy-start = (s32[128]{0:T(128)S(1)}, s32[128]{0:T(128)}, u32[]{:S(2)}) copy-start(s32[128]{0:T(128)} %param.7) | copy-start | bytes 1540
  6.7 1.5 %collective-permute-start = (bf16[2,8,32,128]{3,2,1,0:T(8,128)(2,1)S(1)}, bf16[2,8,32,128]{3,2,1,0:T(8,128)(2,1)S(1)}, u32[]{:S(2)}, u32[]{:S(2)}) collective-permute-start(bf16[2,8,32,128]{3,2,1,0:T(8,128)(2,1)S(1)} %get-tuple-element.8), channel_id=1, source_target_pairs={{0,1},{1,0},{2,3},{3,2},{4,5},{5,4},{6,7},{7,6},{8,9},{9,8},{10,11... | collective-permute-start | bytes 393224 | tf_op jit(solution)/shard_map/ppermute | solution.py:202
  8.2 5.3 %collective-permute-start.1 = (bf16[1,8,32,128]{3,2,1,0:T(8,128)(2,1)S(1)}, bf16[1,8,32,128]{3,2,1,0:T(8,128)(2,1)S(1)}, u32[]{:S(2)}, u32[]{:S(2)}) collective-permute-start(bf16[1,8,32,128]{3,2,1,0:T(8,128)(2,1)S(1)} %add_convert_fusion.1), channel_id=1, source_target_pairs={{0,2},{1,3},{2,0},{3,1},{4,6},{5,7},{6,4},{7,5},{8,10},{9,11},{10,... | collective-permute-start | bytes 196616 | tf_op jit(solution)/shard_map/ppermute | solution.py:202
  13.6 5.3 %collective-permute-start.4 = (bf16[8,32,128]{2,1,0:T(8,128)(2,1)S(1)}, bf16[8,32,128]{2,1,0:T(8,128)(2,1)S(1)}, u32[]{:S(2)}, u32[]{:S(2)}) collective-permute-start(bf16[8,32,128]{2,1,0:T(8,128)(2,1)S(1)} %bitcast.10), channel_id=1, source_target_pairs={{0,16},{4,20},{8,24},{12,28},{16,0},{20,4},{24,8},{28,12},{1,17},{... | collective-permute-start | bytes 196616 | tf_op jit(solution)/shard_map/ppermute | solution.py:202
  18.9 7.9 %collective-permute-start.5 = (bf16[2,8,32,128]{3,2,1,0:T(8,128)(2,1)S(1)}, bf16[2,8,32,128]{3,2,1,0:T(8,128)(2,1)S(1)}, u32[]{:S(2)}, u32[]{:S(2)}) collective-permute-start(bf16[2,8,32,128]{3,2,1,0:T(8,128)(2,1)S(1)} %pad_maximum_fusion), channel_id=1, source_target_pairs={{0,12},{4,8},{8,4},{12,0},{16,28},{20,24},{24,20},{28,16},{1,13},{... | collective-permute-start | bytes 393224 | tf_op jit(solution)/shard_map/ppermute | solution.py:202
  21.8 4.3 %collective-permute-start.3 = (bf16[8,32,128]{2,1,0:T(8,128)(2,1)S(1)}, bf16[8,32,128]{2,1,0:T(8,128)(2,1)S(1)}, u32[]{:S(2)}, u32[]{:S(2)}) collective-permute-start(bf16[8,32,128]{2,1,0:T(8,128)(2,1)S(1)} %bitcast.11), channel_id=1, source_target_pairs={{0,8},{4,12},{8,0},{12,4},{16,24},{20,28},{24,16},{28,20},{1,9},{5... | collective-permute-start | bytes 196616 | tf_op jit(solution)/shard_map/ppermute | solution.py:202
  22.2 4.3 %collective-permute-start.2 = (bf16[8,32,128]{2,1,0:T(8,128)(2,1)S(1)}, bf16[8,32,128]{2,1,0:T(8,128)(2,1)S(1)}, u32[]{:S(2)}, u32[]{:S(2)}) collective-permute-start(bf16[8,32,128]{2,1,0:T(8,128)(2,1)S(1)} %bitcast.12), channel_id=1, source_target_pairs={{0,4},{4,0},{8,12},{12,8},{16,20},{20,16},{24,28},{28,24},{1,5},{5... | collective-permute-start | bytes 196616 | tf_op jit(solution)/shard_map/ppermute | solution.py:202
  22.7 4.3 %collective-permute-start.7 = (bf16[8,32,128]{2,1,0:T(8,128)(2,1)S(1)}, bf16[8,32,128]{2,1,0:T(8,128)(2,1)S(1)}, u32[]{:S(2)}, u32[]{:S(2)}) collective-permute-start(bf16[8,32,128]{2,1,0:T(8,128)(2,1)S(1)} %collective-permute-done.4.refs_3_), channel_id=1, source_target_pairs={{0,8},{4,12},{8,0},{12,4},{16,24},{20,28},{24,16},{28,20},{1,9},{5... | collective-permute-start | bytes 196616 | tf_op jit(solution)/shard_map/ppermute | solution.py:202
  24.6 4.3 %collective-permute-start.6 = (bf16[8,32,128]{2,1,0:T(8,128)(2,1)S(1)}, bf16[8,32,128]{2,1,0:T(8,128)(2,1)S(1)}, u32[]{:S(2)}, u32[]{:S(2)}) collective-permute-start(bf16[8,32,128]{2,1,0:T(8,128)(2,1)S(1)} %collective-permute-done.4.refs_3_), channel_id=1, source_target_pairs={{0,4},{4,0},{8,12},{12,8},{16,20},{20,16},{24,28},{28,24},{1,5},{5... | collective-permute-start | bytes 196616 | tf_op jit(solution)/shard_map/ppermute | solution.py:202

commit v6 on v4

--- a/solution.py
+++ b/solution.py
@@ -157,11 +157,14 @@
     channels = inner // 2
     me, place = me_ref[0], place_ref[:, place_ref.shape[1] // 2 :]
     scale = 1.0 / spectra
+    rows, copies, mine_of = pl.ds(pl.multiple_of(me * local, local), local), [], []
+    mine_place = place_ref[rows, place_ref.shape[1] // 2 :]
     for c in range(channels):
-        row_ref[c] = dot(place, both_parts(blocks, c, channels)).astype(BF16) + early_ref[c]
-    rows, copies = pl.ds(pl.multiple_of(me * local, local), local), []
+        late = both_parts(blocks, c, channels)
+        row_ref[c] = dot(place, late).astype(BF16) + early_ref[c]
+        mine_of.append(dot(mine_place, late).astype(BF16) + early_ref[c, rows, :])
     for c in range(channels):
-        mine = row_ref[c, rows, :]
+        mine = mine_of[c]
         left = jnp.concatenate(
             [mine, jnp.concatenate([mine[:, spectra:], -mine[:, :spectra]], axis=1)], axis=0
         )

time: 30.2 us -> 30.1 us (level)
  no operation moved by 1% of the time
where the time goes in v6:
time: 30.1 us; the launch traced here: 30 us
  starting transfers between devices  13.4 us (45%)
  Pallas kernels  8.25 us (27%)
  waiting for transfers between devices  8.15 us (27%)
    ppermute x8, starting transfers between devices, exchange(): return lax.ppermute(value, axis, [(i, i ^ bit) for i in range(size)])  13.4 us
    ppermute x8, waiting for transfers between devices, exchange(): return lax.ppermute(value, axis, [(i, i ^ bit) for i in range(size)])  8.15 us
    pallas_call x1, Pallas kernels, beam(): pl.pallas_call(functools.partial(beam_kernel, owners), out_shape=(jax.Sha...  6.64 us
    pallas_call x1, Pallas kernels, correlate(): pl.pallas_call(correlate_kernel, out_shape=jax.ShapeDtypeStruct(shape, F3...  1.16 us
  transfers between devices with their start and end apart: 8, of which 6 were waited for; matrix products, arithmetic and copies ran while one was open for 0% of the time, Pallas kernels for 2%

profile of v6, /device:TPU:0, one launch (start us, length us, event | category | flops | bytes accessed | tf_op | source)
XLA Modules:
  0.0 30.0 jit_solution(15576805258219827834)
XLA Ops:
  0.0 0.0 copy-start
  0.0 6.6 %beam.1 = (f32[2,8,32,128]{3,2,1,0:T(8,128)S(1)}, bf16[2,8,32,128]{3,2,1,0:T(8,128)(2,1)S(1)}) custom-call(s32[1]{0:T(128)} %bitcast.2.me_ref, s32[16,64]{1,0:T(8,128)} %index_hbm.1, bf16[2,16,2,16,256]{4,3,2,1,0:T(8,128)(2,1)} %bitcast.16, bf16[2,16,64,2,16,128]{5,4,3,2,1,0:T(8,128)(2,1)} %v_hbm.1), custom_call_target="tpu_custom_call" | custom-call | tf_op jit(solution)/shard_map/beam/pallas_call | solution.py:83
  6.7 0.6 %collective-permute-start = (bf16[2,8,32,128]{3,2,1,0:T(8,128)(2,1)S(1)}, bf16[2,8,32,128]{3,2,1,0:T(8,128)(2,1)S(1)}, u32[]{:S(2)}, u32[]{:S(2)}) collective-permute-start(bf16[2,8,32,128]{3,2,1,0:T(8,128)(2,1)S(1)} %get-tuple-element.8), channel_id=1, source_target_pairs={{0,1},{1,0},{2,3},{3,2},{4,5},{5,4},{6,7},{7,6},{8,9},{9,8},{10,11... | collective-permute-start | bytes 393224 | tf_op jit(solution)/shard_map/ppermute | solution.py:205
  7.2 1.0 %collective-permute-done = bf16[2,8,32,128]{3,2,1,0:T(8,128)(2,1)S(1)} collective-permute-done((bf16[2,8,32,128]{3,2,1,0:T(8,128)(2,1)S(1)}, bf16[2,8,32,128]{3,2,1,0:T(8,128)(2,1)S(1)}, u32[]{:S(2)}, u32[]{:S(2)}) %collective-permute-start) | collective-permute-done | bytes 131104 | tf_op jit(solution)/shard_map/ppermute | solution.py:205
  8.2 2.9 %collective-permute-start.1 = (bf16[1,8,32,128]{3,2,1,0:T(8,128)(2,1)S(1)}, bf16[1,8,32,128]{3,2,1,0:T(8,128)(2,1)S(1)}, u32[]{:S(2)}, u32[]{:S(2)}) collective-permute-start(bf16[1,8,32,128]{3,2,1,0:T(8,128)(2,1)S(1)} %slice.29), channel_id=1, source_target_pairs={{0,2},{1,3},{2,0},{3,1},{4,6},{5,7},{6,4},{7,5},{8,10},{9,11},{10,... | collective-permute-start | bytes 196616 | tf_op jit(solution)/shard_map/ppermute | solution.py:205
  11.2 2.4 %collective-permute-done.1 = bf16[1,8,32,128]{3,2,1,0:T(8,128)(2,1)S(1)} collective-permute-done((bf16[1,8,32,128]{3,2,1,0:T(8,128)(2,1)S(1)}, bf16[1,8,32,128]{3,2,1,0:T(8,128)(2,1)S(1)}, u32[]{:S(2)}, u32[]{:S(2)}) %collective-permute-start.1) | collective-permute-done | bytes 65568 | tf_op jit(solution)/shard_map/ppermute | solution.py:205
  13.6 3.0 %collective-permute-start.4 = (bf16[8,32,128]{2,1,0:T(8,128)(2,1)S(1)}, bf16[8,32,128]{2,1,0:T(8,128)(2,1)S(1)}, u32[]{:S(2)}, u32[]{:S(2)}) collective-permute-start(bf16[8,32,128]{2,1,0:T(8,128)(2,1)S(1)} %bitcast.10), channel_id=1, source_target_pairs={{0,16},{4,20},{8,24},{12,28},{16,0},{20,4},{24,8},{28,12},{1,17},{... | collective-permute-start | bytes 196616 | tf_op jit(solution)/shard_map/ppermute | solution.py:205
  16.6 2.3 %collective-permute-done.4.refs_3_ = bf16[8,32,128]{2,1,0:T(8,128)(2,1)S(1)} collective-permute-done((bf16[8,32,128]{2,1,0:T(8,128)(2,1)S(1)}, bf16[8,32,128]{2,1,0:T(8,128)(2,1)S(1)}, u32[]{:S(2)}, u32[]{:S(2)}) %collective-permute-start.4) | collective-permute-done | bytes 65568 | tf_op jit(solution)/shard_map/ppermute | solution.py:205
  18.9 2.8 %collective-permute-start.5 = (bf16[2,8,32,128]{3,2,1,0:T(8,128)(2,1)S(1)}, bf16[2,8,32,128]{3,2,1,0:T(8,128)(2,1)S(1)}, u32[]{:S(2)}, u32[]{:S(2)}) collective-permute-start(bf16[2,8,32,128]{3,2,1,0:T(8,128)(2,1)S(1)} %pad_maximum_fusion), channel_id=1, source_target_pairs={{0,12},{4,8},{8,4},{12,0},{16,28},{20,24},{24,20},{28,16},{1,13},{... | collective-permute-start | bytes 393224 | tf_op jit(solution)/shard_map/ppermute | solution.py:205
  21.8 0.5 %collective-permute-start.3 = (bf16[8,32,128]{2,1,0:T(8,128)(2,1)S(1)}, bf16[8,32,128]{2,1,0:T(8,128)(2,1)S(1)}, u32[]{:S(2)}, u32[]{:S(2)}) collective-permute-start(bf16[8,32,128]{2,1,0:T(8,128)(2,1)S(1)} %bitcast.11), channel_id=1, source_target_pairs={{0,8},{4,12},{8,0},{12,4},{16,24},{20,28},{24,16},{28,20},{1,9},{5... | collective-permute-start | bytes 196616 | tf_op jit(solution)/shard_map/ppermute | solution.py:205
  22.2 0.3 collective-permute-start.2
  22.5 0.0 copy-done
  22.5 0.2 place.1.place_ref
  22.7 1.9 %collective-permute-start.7 = (bf16[8,32,128]{2,1,0:T(8,128)(2,1)S(1)}, bf16[8,32,128]{2,1,0:T(8,128)(2,1)S(1)}, u32[]{:S(2)}, u32[]{:S(2)}) collective-permute-start(bf16[8,32,128]{2,1,0:T(8,128)(2,1)S(1)} %collective-permute-done.4.refs_3_), channel_id=1, source_target_pairs={{0,8},{4,12},{8,0},{12,4},{16,24},{20,28},{24,16},{28,20},{1,9},{5... | collective-permute-start | bytes 196616 | tf_op jit(solution)/shard_map/ppermute | solution.py:205
  24.6 1.5 %collective-permute-start.6 = (bf16[8,32,128]{2,1,0:T(8,128)(2,1)S(1)}, bf16[8,32,128]{2,1,0:T(8,128)(2,1)S(1)}, u32[]{:S(2)}, u32[]{:S(2)}) collective-permute-start(bf16[8,32,128]{2,1,0:T(8,128)(2,1)S(1)} %collective-permute-done.4.refs_3_), channel_id=1, source_target_pairs={{0,4},{4,0},{8,12},{12,8},{16,20},{20,16},{24,28},{28,24},{1,5},{5... | collective-permute-start | bytes 196616 | tf_op jit(solution)/shard_map/ppermute | solution.py:205
  26.1 0.0 collective-permute-done.3.refs_2_
  26.1 0.4 %collective-permute-done.2.refs_1_ = bf16[8,32,128]{2,1,0:T(8,128)(2,1)S(1)} collective-permute-done((bf16[8,32,128]{2,1,0:T(8,128)(2,1)S(1)}, bf16[8,32,128]{2,1,0:T(8,128)(2,1)S(1)}, u32[]{:S(2)}, u32[]{:S(2)}) %collective-permute-start.2) | collective-permute-done | bytes 65568 | tf_op jit(solution)/shard_map/ppermute | solution.py:205
  26.5 0.3 early.1.early_ref
  26.8 0.0 collective-permute-done.5
  26.8 0.2 collective-permute-done.7.refs_2_
  27.0 1.8 %collective-permute-done.6.refs_1_ = bf16[8,32,128]{2,1,0:T(8,128)(2,1)S(1)} collective-permute-done((bf16[8,32,128]{2,1,0:T(8,128)(2,1)S(1)}, bf16[8,32,128]{2,1,0:T(8,128)(2,1)S(1)}, u32[]{:S(2)}, u32[]{:S(2)}) %collective-permute-start.6) | collective-permute-done | bytes 65568 | tf_op jit(solution)/shard_map/ppermute | solution.py:205
  28.9 1.2 %correlate.1 = f32[4,2,32,256]{3,2,1,0:T(8,128)} custom-call(s32[1]{0:T(128)} %bitcast.me_ref, bf16[256,256]{1,0:T(8,128)(2,1)S(1)} %place.1.place_ref, bf16[4,256,256]{2,1,0:T(8,128)(2,1)S(1)} %early.1.early_ref, bf16[8,32,128]{2,1,0:T(8,128)(2,1)S(1)} %get-tuple-element.10.refs_0_, bf16[8,32,128]{2,1,0:T(8,128)(2,1)S(1)} %collective-permute-done.6.refs_1_, ...), custom_call_target="tpu_custom_call" | custom-call | tf_op jit(solution)/shard_map/correlate/pallas_call | solution.py:185
  (5 shorter events, 0.1 us)
Async XLA Ops:
  0.0 22.5 %copy-start = (s32[128]{0:T(128)S(1)}, s32[128]{0:T(128)}, u32[]{:S(2)}) copy-start(s32[128]{0:T(128)} %param.7) | copy-start | bytes 1540
  6.7 1.5 %collective-permute-start = (bf16[2,8,32,128]{3,2,1,0:T(8,128)(2,1)S(1)}, bf16[2,8,32,128]{3,2,1,0:T(8,128)(2,1)S(1)}, u32[]{:S(2)}, u32[]{:S(2)}) collective-permute-start(bf16[2,8,32,128]{3,2,1,0:T(8,128)(2,1)S(1)} %get-tuple-element.8), channel_id=1, source_target_pairs={{0,1},{1,0},{2,3},{3,2},{4,5},{5,4},{6,7},{7,6},{8,9},{9,8},{10,11... | collective-permute-start | bytes 393224 | tf_op jit(solution)/shard_map/ppermute | solution.py:205
  8.2 5.3 %collective-permute-start.1 = (bf16[1,8,32,128]{3,2,1,0:T(8,128)(2,1)S(1)}, bf16[1,8,32,128]{3,2,1,0:T(8,128)(2,1)S(1)}, u32[]{:S(2)}, u32[]{:S(2)}) collective-permute-start(bf16[1,8,32,128]{3,2,1,0:T(8,128)(2,1)S(1)} %slice.29), channel_id=1, source_target_pairs={{0,2},{1,3},{2,0},{3,1},{4,6},{5,7},{6,4},{7,5},{8,10},{9,11},{10,... | collective-permute-start | bytes 196616 | tf_op jit(solution)/shard_map/ppermute | solution.py:205
  13.6 5.3 %collective-permute-start.4 = (bf16[8,32,128]{2,1,0:T(8,128)(2,1)S(1)}, bf16[8,32,128]{2,1,0:T(8,128)(2,1)S(1)}, u32[]{:S(2)}, u32[]{:S(2)}) collective-permute-start(bf16[8,32,128]{2,1,0:T(8,128)(2,1)S(1)} %bitcast.10), channel_id=1, source_target_pairs={{0,16},{4,20},{8,24},{12,28},{16,0},{20,4},{24,8},{28,12},{1,17},{... | collective-permute-start | bytes 196616 | tf_op jit(solution)/shard_map/ppermute | solution.py:205
  18.9 7.9 %collective-permute-start.5 = (bf16[2,8,32,128]{3,2,1,0:T(8,128)(2,1)S(1)}, bf16[2,8,32,128]{3,2,1,0:T(8,128)(2,1)S(1)}, u32[]{:S(2)}, u32[]{:S(2)}) collective-permute-start(bf16[2,8,32,128]{3,2,1,0:T(8,128)(2,1)S(1)} %pad_maximum_fusion), channel_id=1, source_target_pairs={{0,12},{4,8},{8,4},{12,0},{16,28},{20,24},{24,20},{28,16},{1,13},{... | collective-permute-start | bytes 393224 | tf_op jit(solution)/shard_map/ppermute | solution.py:205
  21.8 4.3 %collective-permute-start.3 = (bf16[8,32,128]{2,1,0:T(8,128)(2,1)S(1)}, bf16[8,32,128]{2,1,0:T(8,128)(2,1)S(1)}, u32[]{:S(2)}, u32[]{:S(2)}) collective-permute-start(bf16[8,32,128]{2,1,0:T(8,128)(2,1)S(1)} %bitcast.11), channel_id=1, source_target_pairs={{0,8},{4,12},{8,0},{12,4},{16,24},{20,28},{24,16},{28,20},{1,9},{5... | collective-permute-start | bytes 196616 | tf_op jit(solution)/shard_map/ppermute | solution.py:205
  22.2 4.3 %collective-permute-start.2 = (bf16[8,32,128]{2,1,0:T(8,128)(2,1)S(1)}, bf16[8,32,128]{2,1,0:T(8,128)(2,1)S(1)}, u32[]{:S(2)}, u32[]{:S(2)}) collective-permute-start(bf16[8,32,128]{2,1,0:T(8,128)(2,1)S(1)} %bitcast.12), channel_id=1, source_target_pairs={{0,4},{4,0},{8,12},{12,8},{16,20},{20,16},{24,28},{28,24},{1,5},{5... | collective-permute-start | bytes 196616 | tf_op jit(solution)/shard_map/ppermute | solution.py:205
  22.7 4.3 %collective-permute-start.7 = (bf16[8,32,128]{2,1,0:T(8,128)(2,1)S(1)}, bf16[8,32,128]{2,1,0:T(8,128)(2,1)S(1)}, u32[]{:S(2)}, u32[]{:S(2)}) collective-permute-start(bf16[8,32,128]{2,1,0:T(8,128)(2,1)S(1)} %collective-permute-done.4.refs_3_), channel_id=1, source_target_pairs={{0,8},{4,12},{8,0},{12,4},{16,24},{20,28},{24,16},{28,20},{1,9},{5... | collective-permute-start | bytes 196616 | tf_op jit(solution)/shard_map/ppermute | solution.py:205
  24.6 4.3 %collective-permute-start.6 = (bf16[8,32,128]{2,1,0:T(8,128)(2,1)S(1)}, bf16[8,32,128]{2,1,0:T(8,128)(2,1)S(1)}, u32[]{:S(2)}, u32[]{:S(2)}) collective-permute-start(bf16[8,32,128]{2,1,0:T(8,128)(2,1)S(1)} %collective-permute-done.4.refs_3_), channel_id=1, source_target_pairs={{0,4},{4,0},{8,12},{12,8},{16,20},{20,16},{24,28},{28,24},{1,5},{5... | collective-permute-start | bytes 196616 | tf_op jit(solution)/shard_map/ppermute | solution.py:205

commit v7 on v4

--- a/solution.py
+++ b/solution.py
@@ -19,12 +19,12 @@
     return jnp.dot(left, right, preferred_element_type=F32)
 
 
-def beam_kernel(owners, me_ref, index_hbm, w_hbm, v_hbm, keep_ref, send_ref, index_ref, w_ref, v_ref, left_ref, acc_ref, small_sem, v_sem):
+def beam_kernel(owners, index_hbm, w_hbm, v_hbm, keep_ref, send_ref, index_ref, w_ref, v_ref, left_ref, acc_ref, small_sem, v_sem):
     _, stations, antennas, polars, channels, spectra = v_ref.shape
     numbers = w_ref.shape[-1]
     per_owner = channels // owners
     rows = 2 * channels
-    me = me_ref[0]
+    me = lax.axis_index("tile").astype(jnp.int32)
     copies = [pltpu.make_async_copy(index_hbm, index_ref, small_sem.at[0]), pltpu.make_async_copy(w_hbm, w_ref, small_sem.at[1])]
     spans = [(s, min(s + 2, stations)) for s in range(0, stations - 2, 2)] + [(s, s + 1) for s in range(max(stations - 2, 0), stations)]
     arrivals = {a: pltpu.make_async_copy(v_hbm.at[:, a:b], v_ref.at[:, a:b], v_sem.at[a]) for a, b in spans}
@@ -75,7 +75,7 @@
             order_rows(s + 1, batch)
 
 
-def beam(owners, me, index, weights, voltages):
+def beam(owners, index, weights, voltages):
     _, stations, antennas, polars, channels, spectra = voltages.shape
     rows = 2 * channels
     half = (owners // 2, rows // owners, stations * polars, spectra)
@@ -83,7 +83,7 @@
     return pl.pallas_call(
         functools.partial(beam_kernel, owners),
         out_shape=(jax.ShapeDtypeStruct(half, F32), jax.ShapeDtypeStruct(half, BF16)),
-        in_specs=[pl.BlockSpec(memory_space=pltpu.SMEM), hbm, hbm, hbm],
+        in_specs=[hbm, hbm, hbm],
         out_specs=[vmem, vmem],
         scratch_shapes=[
             pltpu.VMEM(index.shape, jnp.int32),
@@ -96,32 +96,32 @@
         ],
         compiler_params=pltpu.CompilerParams(vmem_limit_bytes=48 << 20),
         name="beam",
-    )(me, *(pltpu.with_memory_space_constraint(a, pltpu.HBM) for a in (index, weights, voltages)))
-
-
-def place_kernel(local, polars, me_ref, order_ref, place_ref):
+    )(*(pltpu.with_memory_space_constraint(a, pltpu.HBM) for a in (index, weights, voltages)))
+
+
+def place_kernel(local, polars, order_ref, place_ref):
     total, stations = place_ref.shape[0], order_ref.shape[1]
     owns = jnp.where(order_ref[...] == iota((total, stations), 0) // polars, 1.0, 0.0).astype(BF16)
     column = iota((stations, total), 1)
     block, far = column // local, total // local // 2
     block = jnp.where(block == far, far - 1, jnp.where(block == far - 1, far, block))
-    slot = (block ^ me_ref[0]) * (local // polars) + (column % local) // polars
+    slot = (block ^ lax.axis_index("sgroup").astype(jnp.int32)) * (local // polars) + (column % local) // polars
     slots = jnp.where(iota((stations, total), 0) == slot, 1.0, 0.0).astype(BF16)
     same = iota((total, total), 0) % polars == iota((total, total), 1) % polars
     place_ref[...] = jnp.where(same, dot(owns, slots), 0.0).astype(BF16)
 
 
-def placement(me, order, polars, local):
+def placement(order, polars, local):
     vmem = pl.BlockSpec(memory_space=pltpu.VMEM)
     total = order.shape[0] * polars
     return pl.pallas_call(
         functools.partial(place_kernel, local, polars),
         out_shape=jax.ShapeDtypeStruct((total, total), BF16),
-        in_specs=[pl.BlockSpec(memory_space=pltpu.SMEM), vmem],
+        in_specs=[vmem],
         out_specs=vmem,
         compiler_params=pltpu.CompilerParams(vmem_limit_bytes=48 << 20),
         name="place",
-    )(me, order[None, :])
+    )(order[None, :])
 
 
 def both_parts(blocks, c, channels):
@@ -151,11 +151,11 @@
     )(place, *blocks)
 
 
-def correlate_kernel(me_ref, place_ref, early_ref, *refs):
+def correlate_kernel(place_ref, early_ref, *refs):
     blocks, (out_hbm, row_ref, out_ref, sem) = refs[:-4], refs[-4:]
     inner, local, spectra = blocks[0].shape
     channels = inner // 2
-    me, place = me_ref[0], place_ref[:, place_ref.shape[1] // 2 :]
+    me, place = lax.axis_index("sgroup").astype(jnp.int32), place_ref[:, place_ref.shape[1] // 2 :]
     scale = 1.0 / spectra
     for c in range(channels):
         row_ref[c] = dot(place, both_parts(blocks, c, channels)).astype(BF16) + early_ref[c]
@@ -174,7 +174,7 @@
         copy.wait()
 
 
-def correlate(me, place, ordered, blocks):
+def correlate(place, ordered, blocks):
     inner, local, spectra = blocks[0].shape
     total = place.shape[0]
     shape = (inner // 2, 2, local, total)
@@ -182,7 +182,7 @@
     return pl.pallas_call(
         correlate_kernel,
         out_shape=jax.ShapeDtypeStruct(shape, F32),
-        in_specs=[pl.BlockSpec(memory_space=pltpu.SMEM)] + [vmem] * (2 + len(blocks)),
+        in_specs=[vmem] * (2 + len(blocks)),
         out_specs=pl.BlockSpec(memory_space=pltpu.HBM),
         scratch_shapes=[
             pltpu.VMEM((inner // 2, total, 2 * spectra), BF16),
@@ -191,11 +191,10 @@
         ],
         compiler_params=pltpu.CompilerParams(vmem_limit_bytes=48 << 20),
         name="correlate",
-    )(me, place, ordered, *blocks)
+    )(place, ordered, *blocks)
 
 
 def body(groups, owners, voltages, weights, antenna_slot_index, station_order):
-    group, tile = lax.axis_index("sgroup").astype(jnp.int32), lax.axis_index("tile").astype(jnp.int32)
     far = groups // 2
 
     def exchange(value, axis, size, bit):
@@ -204,7 +203,7 @@
     def share(value, bit):
         return exchange(value, "sgroup", groups, bit)
 
-    keep, send = beam(owners, tile[None], antenna_slot_index, jnp.transpose(weights, (0, 1, 3, 4, 2)), voltages)
+    keep, send = beam(owners, antenna_slot_index, jnp.transpose(weights, (0, 1, 3, 4, 2)), voltages)
     total = keep + exchange(send, "tile", owners, 1).astype(F32)
     bit = 2
     while bit < owners:
@@ -220,10 +219,10 @@
     blocks[far - 1], blocks[far + far - 1] = both[0], both[1]
     for i in range(1, far - 1):
         blocks[far + i] = share(blocks[far], i)
-    place = placement(group[None], station_order, voltages.shape[3], own.shape[1])
+    place = placement(station_order, voltages.shape[3], own.shape[1])
     first = [*range(far - 1), far]
     ordered = early(place, [blocks[i] for i in first])
-    return correlate(group[None], place, ordered, [blocks[i] for i in range(groups) if i not in first])
+    return correlate(place, ordered, [blocks[i] for i in range(groups) if i not in first])
 
 
 def solution(mesh):

time: 30.2 us -> 30.2 us (level)
  no operation moved by 1% of the time
where the time goes in v7:
time: 30.2 us; the launch traced here: 30 us
  starting transfers between devices  13.5 us (45%)
  Pallas kernels  8.29 us (27%)
  waiting for transfers between devices  8.14 us (27%)
    ppermute x8, starting transfers between devices, exchange(): return lax.ppermute(value, axis, [(i, i ^ bit) for i in range(size)])  13.5 us
    ppermute x8, waiting for transfers between devices, exchange(): return lax.ppermute(value, axis, [(i, i ^ bit) for i in range(size)])  8.14 us
    pallas_call x1, Pallas kernels, beam(): pl.pallas_call(functools.partial(beam_kernel, owners), out_shape=(jax.Sha...  6.63 us
    pallas_call x1, Pallas kernels, correlate(): pl.pallas_call(correlate_kernel, out_shape=jax.ShapeDtypeStruct(shape, F3...  1.19 us
  transfers between devices with their start and end apart: 8, of which 6 were waited for; matrix products, arithmetic and copies ran while one was open for 0% of the time, Pallas kernels for 2%

profile of v7, /device:TPU:0, one launch (start us, length us, event | category | flops | bytes accessed | tf_op | source)
XLA Modules:
  0.0 30.0 jit_solution(7260121058674271821)
XLA Ops:
  0.0 0.0 copy-start
  0.0 6.6 %beam.1 = (f32[2,8,32,128]{3,2,1,0:T(8,128)S(1)}, bf16[2,8,32,128]{3,2,1,0:T(8,128)(2,1)S(1)}) custom-call(s32[16,64]{1,0:T(8,128)} %index_hbm.1, bf16[2,16,2,16,256]{4,3,2,1,0:T(8,128)(2,1)} %bitcast.14, bf16[2,16,64,2,16,128]{5,4,3,2,1,0:T(8,128)(2,1)} %v_hbm.1), custom_call_target="tpu_custom_call" | custom-call | tf_op jit(solution)/shard_map/beam/pallas_call | solution.py:83
  6.6 0.6 %collective-permute-start = (bf16[2,8,32,128]{3,2,1,0:T(8,128)(2,1)S(1)}, bf16[2,8,32,128]{3,2,1,0:T(8,128)(2,1)S(1)}, u32[]{:S(2)}, u32[]{:S(2)}) collective-permute-start(bf16[2,8,32,128]{3,2,1,0:T(8,128)(2,1)S(1)} %get-tuple-element.8), channel_id=1, source_target_pairs={{0,1},{1,0},{2,3},{3,2},{4,5},{5,4},{6,7},{7,6},{8,9},{9,8},{10,11... | collective-permute-start | bytes 393224 | tf_op jit(solution)/shard_map/ppermute | solution.py:201
  7.2 1.0 %collective-permute-done = bf16[2,8,32,128]{3,2,1,0:T(8,128)(2,1)S(1)} collective-permute-done((bf16[2,8,32,128]{3,2,1,0:T(8,128)(2,1)S(1)}, bf16[2,8,32,128]{3,2,1,0:T(8,128)(2,1)S(1)}, u32[]{:S(2)}, u32[]{:S(2)}) %collective-permute-start) | collective-permute-done | bytes 131104 | tf_op jit(solution)/shard_map/ppermute | solution.py:201
  8.2 2.9 %collective-permute-start.1 = (bf16[1,8,32,128]{3,2,1,0:T(8,128)(2,1)S(1)}, bf16[1,8,32,128]{3,2,1,0:T(8,128)(2,1)S(1)}, u32[]{:S(2)}, u32[]{:S(2)}) collective-permute-start(bf16[1,8,32,128]{3,2,1,0:T(8,128)(2,1)S(1)} %slice.29), channel_id=1, source_target_pairs={{0,2},{1,3},{2,0},{3,1},{4,6},{5,7},{6,4},{7,5},{8,10},{9,11},{10,... | collective-permute-start | bytes 196616 | tf_op jit(solution)/shard_map/ppermute | solution.py:201
  11.2 2.4 %collective-permute-done.1 = bf16[1,8,32,128]{3,2,1,0:T(8,128)(2,1)S(1)} collective-permute-done((bf16[1,8,32,128]{3,2,1,0:T(8,128)(2,1)S(1)}, bf16[1,8,32,128]{3,2,1,0:T(8,128)(2,1)S(1)}, u32[]{:S(2)}, u32[]{:S(2)}) %collective-permute-start.1) | collective-permute-done | bytes 65568 | tf_op jit(solution)/shard_map/ppermute | solution.py:201
  13.6 3.0 %collective-permute-start.4 = (bf16[8,32,128]{2,1,0:T(8,128)(2,1)S(1)}, bf16[8,32,128]{2,1,0:T(8,128)(2,1)S(1)}, u32[]{:S(2)}, u32[]{:S(2)}) collective-permute-start(bf16[8,32,128]{2,1,0:T(8,128)(2,1)S(1)} %bitcast.8), channel_id=1, source_target_pairs={{0,16},{4,20},{8,24},{12,28},{16,0},{20,4},{24,8},{28,12},{1,17},{... | collective-permute-start | bytes 196616 | tf_op jit(solution)/shard_map/ppermute | solution.py:201
  16.6 2.3 %collective-permute-done.4.refs_3_ = bf16[8,32,128]{2,1,0:T(8,128)(2,1)S(1)} collective-permute-done((bf16[8,32,128]{2,1,0:T(8,128)(2,1)S(1)}, bf16[8,32,128]{2,1,0:T(8,128)(2,1)S(1)}, u32[]{:S(2)}, u32[]{:S(2)}) %collective-permute-start.4) | collective-permute-done | bytes 65568 | tf_op jit(solution)/shard_map/ppermute | solution.py:201
  18.9 2.9 %collective-permute-start.5 = (bf16[2,8,32,128]{3,2,1,0:T(8,128)(2,1)S(1)}, bf16[2,8,32,128]{3,2,1,0:T(8,128)(2,1)S(1)}, u32[]{:S(2)}, u32[]{:S(2)}) collective-permute-start(bf16[2,8,32,128]{3,2,1,0:T(8,128)(2,1)S(1)} %pad_maximum_fusion), channel_id=1, source_target_pairs={{0,12},{4,8},{8,4},{12,0},{16,28},{20,24},{24,20},{28,16},{1,13},{... | collective-permute-start | bytes 393224 | tf_op jit(solution)/shard_map/ppermute | solution.py:201
  21.8 0.4 %collective-permute-start.3 = (bf16[8,32,128]{2,1,0:T(8,128)(2,1)S(1)}, bf16[8,32,128]{2,1,0:T(8,128)(2,1)S(1)}, u32[]{:S(2)}, u32[]{:S(2)}) collective-permute-start(bf16[8,32,128]{2,1,0:T(8,128)(2,1)S(1)} %bitcast.9), channel_id=1, source_target_pairs={{0,8},{4,12},{8,0},{12,4},{16,24},{20,28},{24,16},{28,20},{1,9},{5... | collective-permute-start | bytes 196616 | tf_op jit(solution)/shard_map/ppermute | solution.py:201
  22.2 0.2 collective-permute-start.2
  22.5 0.0 copy-done
  22.5 0.2 place.1.place_ref
  22.7 1.9 %collective-permute-start.7 = (bf16[8,32,128]{2,1,0:T(8,128)(2,1)S(1)}, bf16[8,32,128]{2,1,0:T(8,128)(2,1)S(1)}, u32[]{:S(2)}, u32[]{:S(2)}) collective-permute-start(bf16[8,32,128]{2,1,0:T(8,128)(2,1)S(1)} %collective-permute-done.4.refs_3_), channel_id=1, source_target_pairs={{0,8},{4,12},{8,0},{12,4},{16,24},{20,28},{24,16},{28,20},{1,9},{5... | collective-permute-start | bytes 196616 | tf_op jit(solution)/shard_map/ppermute | solution.py:201
  24.6 1.5 %collective-permute-start.6 = (bf16[8,32,128]{2,1,0:T(8,128)(2,1)S(1)}, bf16[8,32,128]{2,1,0:T(8,128)(2,1)S(1)}, u32[]{:S(2)}, u32[]{:S(2)}) collective-permute-start(bf16[8,32,128]{2,1,0:T(8,128)(2,1)S(1)} %collective-permute-done.4.refs_3_), channel_id=1, source_target_pairs={{0,4},{4,0},{8,12},{12,8},{16,20},{20,16},{24,28},{28,24},{1,5},{5... | collective-permute-start | bytes 196616 | tf_op jit(solution)/shard_map/ppermute | solution.py:201
  26.1 0.0 collective-permute-done.3.refs_2_
  26.1 0.4 %collective-permute-done.2.refs_1_ = bf16[8,32,128]{2,1,0:T(8,128)(2,1)S(1)} collective-permute-done((bf16[8,32,128]{2,1,0:T(8,128)(2,1)S(1)}, bf16[8,32,128]{2,1,0:T(8,128)(2,1)S(1)}, u32[]{:S(2)}, u32[]{:S(2)}) %collective-permute-start.2) | collective-permute-done | bytes 65568 | tf_op jit(solution)/shard_map/ppermute | solution.py:201
  26.5 0.3 early.1.early_ref
  26.8 0.0 collective-permute-done.5
  26.8 0.2 collective-permute-done.7.refs_2_
  27.0 1.8 %collective-permute-done.6.refs_1_ = bf16[8,32,128]{2,1,0:T(8,128)(2,1)S(1)} collective-permute-done((bf16[8,32,128]{2,1,0:T(8,128)(2,1)S(1)}, bf16[8,32,128]{2,1,0:T(8,128)(2,1)S(1)}, u32[]{:S(2)}, u32[]{:S(2)}) %collective-permute-start.6) | collective-permute-done | bytes 65568 | tf_op jit(solution)/shard_map/ppermute | solution.py:201
  28.9 1.2 %correlate.1 = f32[4,2,32,256]{3,2,1,0:T(8,128)} custom-call(bf16[256,256]{1,0:T(8,128)(2,1)S(1)} %place.1.place_ref, bf16[4,256,256]{2,1,0:T(8,128)(2,1)S(1)} %early.1.early_ref, bf16[8,32,128]{2,1,0:T(8,128)(2,1)S(1)} %get-tuple-element.10.refs_0_, bf16[8,32,128]{2,1,0:T(8,128)(2,1)S(1)} %collective-permute-done.6.refs_1_, ...), custom_call_target="tpu_custom_call" | custom-call | tf_op jit(solution)/shard_map/correlate/pallas_call | solution.py:182
  (5 shorter events, 0.1 us)
Async XLA Ops:
  0.0 22.5 %copy-start = (s32[128]{0:T(128)S(1)}, s32[128]{0:T(128)}, u32[]{:S(2)}) copy-start(s32[128]{0:T(128)} %param.7) | copy-start | bytes 1540
  6.6 1.5 %collective-permute-start = (bf16[2,8,32,128]{3,2,1,0:T(8,128)(2,1)S(1)}, bf16[2,8,32,128]{3,2,1,0:T(8,128)(2,1)S(1)}, u32[]{:S(2)}, u32[]{:S(2)}) collective-permute-start(bf16[2,8,32,128]{3,2,1,0:T(8,128)(2,1)S(1)} %get-tuple-element.8), channel_id=1, source_target_pairs={{0,1},{1,0},{2,3},{3,2},{4,5},{5,4},{6,7},{7,6},{8,9},{9,8},{10,11... | collective-permute-start | bytes 393224 | tf_op jit(solution)/shard_map/ppermute | solution.py:201
  8.2 5.3 %collective-permute-start.1 = (bf16[1,8,32,128]{3,2,1,0:T(8,128)(2,1)S(1)}, bf16[1,8,32,128]{3,2,1,0:T(8,128)(2,1)S(1)}, u32[]{:S(2)}, u32[]{:S(2)}) collective-permute-start(bf16[1,8,32,128]{3,2,1,0:T(8,128)(2,1)S(1)} %slice.29), channel_id=1, source_target_pairs={{0,2},{1,3},{2,0},{3,1},{4,6},{5,7},{6,4},{7,5},{8,10},{9,11},{10,... | collective-permute-start | bytes 196616 | tf_op jit(solution)/shard_map/ppermute | solution.py:201
  13.6 5.3 %collective-permute-start.4 = (bf16[8,32,128]{2,1,0:T(8,128)(2,1)S(1)}, bf16[8,32,128]{2,1,0:T(8,128)(2,1)S(1)}, u32[]{:S(2)}, u32[]{:S(2)}) collective-permute-start(bf16[8,32,128]{2,1,0:T(8,128)(2,1)S(1)} %bitcast.8), channel_id=1, source_target_pairs={{0,16},{4,20},{8,24},{12,28},{16,0},{20,4},{24,8},{28,12},{1,17},{... | collective-permute-start | bytes 196616 | tf_op jit(solution)/shard_map/ppermute | solution.py:201
  18.9 7.9 %collective-permute-start.5 = (bf16[2,8,32,128]{3,2,1,0:T(8,128)(2,1)S(1)}, bf16[2,8,32,128]{3,2,1,0:T(8,128)(2,1)S(1)}, u32[]{:S(2)}, u32[]{:S(2)}) collective-permute-start(bf16[2,8,32,128]{3,2,1,0:T(8,128)(2,1)S(1)} %pad_maximum_fusion), channel_id=1, source_target_pairs={{0,12},{4,8},{8,4},{12,0},{16,28},{20,24},{24,20},{28,16},{1,13},{... | collective-permute-start | bytes 393224 | tf_op jit(solution)/shard_map/ppermute | solution.py:201
  21.8 4.3 %collective-permute-start.3 = (bf16[8,32,128]{2,1,0:T(8,128)(2,1)S(1)}, bf16[8,32,128]{2,1,0:T(8,128)(2,1)S(1)}, u32[]{:S(2)}, u32[]{:S(2)}) collective-permute-start(bf16[8,32,128]{2,1,0:T(8,128)(2,1)S(1)} %bitcast.9), channel_id=1, source_target_pairs={{0,8},{4,12},{8,0},{12,4},{16,24},{20,28},{24,16},{28,20},{1,9},{5... | collective-permute-start | bytes 196616 | tf_op jit(solution)/shard_map/ppermute | solution.py:201
  22.2 4.3 %collective-permute-start.2 = (bf16[8,32,128]{2,1,0:T(8,128)(2,1)S(1)}, bf16[8,32,128]{2,1,0:T(8,128)(2,1)S(1)}, u32[]{:S(2)}, u32[]{:S(2)}) collective-permute-start(bf16[8,32,128]{2,1,0:T(8,128)(2,1)S(1)} %bitcast.10), channel_id=1, source_target_pairs={{0,4},{4,0},{8,12},{12,8},{16,20},{20,16},{24,28},{28,24},{1,5},{5... | collective-permute-start | bytes 196616 | tf_op jit(solution)/shard_map/ppermute | solution.py:201
  22.7 4.3 %collective-permute-start.7 = (bf16[8,32,128]{2,1,0:T(8,128)(2,1)S(1)}, bf16[8,32,128]{2,1,0:T(8,128)(2,1)S(1)}, u32[]{:S(2)}, u32[]{:S(2)}) collective-permute-start(bf16[8,32,128]{2,1,0:T(8,128)(2,1)S(1)} %collective-permute-done.4.refs_3_), channel_id=1, source_target_pairs={{0,8},{4,12},{8,0},{12,4},{16,24},{20,28},{24,16},{28,20},{1,9},{5... | collective-permute-start | bytes 196616 | tf_op jit(solution)/shard_map/ppermute | solution.py:201
  24.6 4.3 %collective-permute-start.6 = (bf16[8,32,128]{2,1,0:T(8,128)(2,1)S(1)}, bf16[8,32,128]{2,1,0:T(8,128)(2,1)S(1)}, u32[]{:S(2)}, u32[]{:S(2)}) collective-permute-start(bf16[8,32,128]{2,1,0:T(8,128)(2,1)S(1)} %collective-permute-done.4.refs_3_), channel_id=1, source_target_pairs={{0,4},{4,0},{8,12},{12,8},{16,20},{20,16},{24,28},{28,24},{1,5},{5... | collective-permute-start | bytes 196616 | tf_op jit(solution)/shard_map/ppermute | solution.py:201
